TPU v7x, 32 devices: a whole 2x2x4 slice. The times are simulated.
32 devices in a mesh: wide: 4 (over z), narrow: 8 (over y, x, core).
Axes of the slice: x: 2, y: 2, z: 4, core: 2. Of those that a mesh axis runs over, the one named last changes fastest.
Arguments:
- sources: bfloat16 [32768, 768], P(('wide', 'narrow')), as said below
- targets: bfloat16 [32768, 768], P(('wide', 'narrow')), as said below
- target_lists: int32 [256, 4], P(('wide', 'narrow')), may hold values from 0 to 255, as said below
- target_clusters: int32 [32768], P(('wide', 'narrow')), may hold values from 0 to 8191
- centroids_src: bfloat16 [8192, 768], P(('wide', 'narrow')), may hold values from -6 to 6
- centroids_tgt: bfloat16 [8192, 768], P('narrow', 'wide'), may hold values from -6 to 6
- sender_mean_measure: float32 [8192], P('wide'), may hold values from 0.05 to 20
- recipient_mean_measure: float32 [8192], P('narrow'), may hold values from 0.05 to 20
Outputs:
- src_bary: bfloat16 [32768, 768], P(('wide', 'narrow'))
- tgt_bary: bfloat16 [32768, 768], P(('wide', 'narrow'))
- src_potential: float32 [32768], P(('wide', 'narrow'))
- tgt_potential: float32 [32768], P(('wide', 'narrow'))
Inputs may be any that keep to these rules, and one draw needn't show every extreme that they name: `target_lists`: target block t holds targets t * 128 to (t + 1) * 128 - 1. Every entry names a block held by a device with the same wide index as the device of the source block. Among the 32 entries of one device, at most 5 name blocks held by any one device, and on every device some device is named by exactly 5. Every target block is named by at least one entry. `sources`: Real-valued features. `targets`: Real-valued features.
All inputs are finite; a program needn't handle non-finite values.
Results may differ from a plain program's by a relative error of at most 0.007.
Values may be sent and summed in bfloat16 or wider, within the bound.
A program may use at most 128 MiB of HBM per device.

v0:
```python
import jax
import jax.numpy as jnp
from jax import lax
from jax.sharding import PartitionSpec as P

BLK = 128
LIST = 4
ITC = 6
STEPS = 3


heat_parameter = 0.02


def contract_rows(left_rows, right_rows):
    return lax.dot_general(
        left_rows, right_rows, (((1,), (1,)), ((), ())), preferred_element_type=jnp.float32
    )


def square_norms(rows_in):
    return jnp.sum(jnp.square(rows_in.astype(jnp.float32)), axis=-1)


def lateral_lse_offset(rating_grid_form):
    best_rating = lax.pmax(jnp.max(rating_grid_form, axis=1), "narrow")
    ongoing_additions = lax.psum(
        jnp.sum(jnp.exp(rating_grid_form - best_rating[:, None]), axis=1), "narrow"
    )
    return best_rating + jnp.log(ongoing_additions)


def vertical_lse_offset(rating_grid_form):
    best_rating = lax.pmax(jnp.max(rating_grid_form, axis=0), "wide")
    ongoing_additions = lax.psum(
        jnp.sum(jnp.exp(rating_grid_form - best_rating[None, :]), axis=0), "wide"
    )
    return best_rating + jnp.log(ongoing_additions)


def body(
    sources,
    targets,
    target_lists,
    target_clusters,
    centroids_src,
    centroids_tgt,
    sender_mean_measure,
    recipient_mean_measure,
):
    feature_count = sources.shape[1]
    narrow_count = lax.axis_size("narrow")
    col_panel = lax.all_gather(centroids_tgt, "wide", axis=1, tiled=True)
    col_sq = square_norms(col_panel)
    fragment = lax.all_gather(centroids_src, "narrow", axis=0, tiled=True)
    blurred_stratum = (
        square_norms(fragment)[:, None] + col_sq[None, :] - 2.0 * contract_rows(fragment, col_panel)
    ) / feature_count
    ln_sender_measure = heat_parameter * jnp.log(sender_mean_measure)
    ln_recipient_measure = heat_parameter * jnp.log(recipient_mean_measure)

    def coarse_turn(iteration, recipient_blurred_stratum):
        sender_blurred_stratum = ln_sender_measure - heat_parameter * lateral_lse_offset(
            (recipient_blurred_stratum[None, :] - blurred_stratum) / heat_parameter
        )
        return ln_recipient_measure - heat_parameter * vertical_lse_offset(
            (sender_blurred_stratum[:, None] - blurred_stratum) / heat_parameter
        )

    coarse_cols = lax.fori_loop(
        0, ITC, coarse_turn, jnp.zeros((blurred_stratum.shape[1],), jnp.float32)
    )
    coarse_all = lax.all_gather(coarse_cols, "narrow", axis=0, tiled=True)
    src_blocks = sources.reshape(-1, BLK, feature_count)
    tgt_blocks = targets.reshape(-1, BLK, feature_count)
    src_count = src_blocks.shape[0]
    tgt_count = tgt_blocks.shape[0]
    capacity = max(
        (5 * src_count * LIST + 4 * narrow_count - 1) // (4 * narrow_count),
        (tgt_count + narrow_count - 1) // narrow_count,
    )
    slot_count = narrow_count * capacity
    wanted = target_lists.reshape(-1)
    entries = wanted.shape[0]
    entry_index = jnp.arange(entries, dtype=jnp.int32)
    owner_of = wanted // tgt_count % narrow_count
    local_block = wanted % tgt_count
    earlier = jnp.logical_and(
        owner_of[:, None] == owner_of[None, :], entry_index[None, :] < entry_index[:, None]
    )
    rank_of = jnp.sum(earlier.astype(jnp.int32), axis=1)
    slot_of = owner_of * capacity + rank_of
    requests = (
        jnp.full((slot_count,), -1, jnp.int32)
        .at[slot_of]
        .set(local_block)
        .reshape(narrow_count, capacity)
    )

    def into_slots(values):
        return jnp.zeros((slot_count,) + values.shape[1:], values.dtype).at[slot_of].set(values)

    asked_ids = lax.all_to_all(requests, "narrow", split_axis=0, concat_axis=0, tiled=True)
    found = jnp.take(tgt_blocks, jnp.clip(asked_ids, 0, tgt_count - 1), axis=0)
    received, asked_ids = (
        lax.all_to_all(
            jnp.where((asked_ids >= 0)[:, :, None, None], found, jnp.zeros((), jnp.bfloat16)),
            "narrow",
            split_axis=0,
            concat_axis=0,
            tiled=True,
        ),
        asked_ids,
    )
    rows_entry = jnp.take(
        received.reshape(slot_count, BLK, feature_count), slot_of, axis=0
    ).reshape(src_count, LIST, BLK, feature_count)
    src_sq = square_norms(src_blocks)
    rows_sq = square_norms(rows_entry)
    cross_term = jnp.einsum(
        "bid,blcd->blic", src_blocks, rows_entry, preferred_element_type=jnp.float32
    )
    pointwise_charge = (
        src_sq[:, None, :, None] + rows_sq[:, :, None, :] - 2.0 * cross_term
    ) / feature_count
    flat_asked = asked_ids.reshape(-1)
    slot_live = flat_asked >= 0
    clipped_asked = jnp.clip(flat_asked, 0, tgt_count - 1)
    slot_pick = flat_asked[None, :] == jnp.arange(tgt_count, dtype=jnp.int32)[:, None]
    recipient_kantorovich = jnp.take(coarse_all, target_clusters, axis=0).reshape(tgt_count, BLK)

    def send_potentials(values):
        outgoing = jnp.where(
            slot_live[:, None], jnp.take(values, clipped_asked, axis=0), 0.0
        ).reshape(narrow_count, capacity, BLK)
        back = lax.all_to_all(outgoing, "narrow", split_axis=0, concat_axis=0, tiled=True)
        return jnp.take(back.reshape(slot_count, BLK), slot_of, axis=0).reshape(
            src_count, LIST, BLK
        )

    sender_kantorovich = jnp.zeros((src_count, BLK), jnp.float32)
    for iteration in range(STEPS):
        named_kantorovich = send_potentials(recipient_kantorovich)
        rating_grid_form = (named_kantorovich[:, :, None, :] - pointwise_charge) / heat_parameter
        best_rating = jnp.max(rating_grid_form, axis=(1, 3))
        sender_kantorovich = -heat_parameter * (
            best_rating
            + jnp.log(
                jnp.sum(jnp.exp(rating_grid_form - best_rating[:, None, :, None]), axis=(1, 3))
            )
        )
        reverse_score_matrix = (
            sender_kantorovich[:, None, :, None] - pointwise_charge
        ) / heat_parameter
        part_top = jnp.max(reverse_score_matrix, axis=2)
        part_sum = jnp.sum(jnp.exp(reverse_score_matrix - part_top[:, :, None, :]), axis=2)
        top_slots = into_slots(part_top.reshape(entries, BLK)).reshape(narrow_count, capacity, BLK)
        sum_slots = into_slots(part_sum.reshape(entries, BLK)).reshape(narrow_count, capacity, BLK)
        top_back, sum_back = (
            lax.all_to_all(top_slots, "narrow", split_axis=0, concat_axis=0, tiled=True),
            lax.all_to_all(sum_slots, "narrow", split_axis=0, concat_axis=0, tiled=True),
        )
        flat_top = top_back.reshape(slot_count, BLK)
        flat_sum = sum_back.reshape(slot_count, BLK)
        largest_figure = jnp.max(
            jnp.where(slot_pick[:, :, None], flat_top[None, :, :], -jnp.inf), axis=1
        )
        ongoing_additions = jnp.sum(
            jnp.where(
                slot_pick[:, :, None],
                flat_sum[None, :, :] * jnp.exp(flat_top[None, :, :] - largest_figure[:, None, :]),
                0.0,
            ),
            axis=1,
        )
        recipient_kantorovich = -heat_parameter * (largest_figure + jnp.log(ongoing_additions))
    named_kantorovich = send_potentials(recipient_kantorovich)
    joint_measure_shares_entrywise = jnp.exp(
        (sender_kantorovich[:, None, :, None] + named_kantorovich[:, :, None, :] - pointwise_charge)
        / heat_parameter
    ).astype(jnp.bfloat16)
    src_num = jnp.einsum(
        "blic,blcd->bid",
        joint_measure_shares_entrywise,
        rows_entry,
        preferred_element_type=jnp.float32,
    )
    src_den = jnp.sum(joint_measure_shares_entrywise, axis=(1, 3), dtype=jnp.float32)
    src_bary = (src_num / src_den[:, :, None]).astype(jnp.bfloat16).reshape(-1, feature_count)
    entry_rows = jnp.einsum(
        "blic,bid->blcd",
        joint_measure_shares_entrywise,
        src_blocks,
        preferred_element_type=jnp.float32,
    ).astype(jnp.bfloat16)
    entry_mass = jnp.sum(joint_measure_shares_entrywise, axis=2, dtype=jnp.float32).astype(
        jnp.bfloat16
    )
    row_slots = into_slots(entry_rows.reshape(entries, BLK, feature_count)).reshape(
        narrow_count, capacity, BLK, feature_count
    )
    mass_slots = into_slots(entry_mass.reshape(entries, BLK)).reshape(narrow_count, capacity, BLK)
    numerator, denominator = (
        lax.all_to_all(row_slots, "narrow", split_axis=0, concat_axis=0, tiled=True),
        lax.all_to_all(mass_slots, "narrow", split_axis=0, concat_axis=0, tiled=True),
    )
    numerator = numerator.reshape(slot_count, BLK, feature_count)
    denominator = denominator.reshape(slot_count, BLK)
    picker = slot_pick.astype(jnp.bfloat16)
    tgt_num = jnp.dot(
        picker,
        numerator.reshape(slot_count, BLK * feature_count),
        preferred_element_type=jnp.float32,
    ).reshape(tgt_count, BLK, feature_count)
    tgt_den = jnp.dot(picker, denominator, preferred_element_type=jnp.float32)
    tgt_bary = (tgt_num / tgt_den[:, :, None]).astype(jnp.bfloat16).reshape(-1, feature_count)
    return (src_bary, tgt_bary, sender_kantorovich.reshape(-1), recipient_kantorovich.reshape(-1))


def solution(mesh):
    in_specs = (
        P(("wide", "narrow"), None),
        P(("wide", "narrow"), None),
        P(("wide", "narrow"), None),
        P(("wide", "narrow")),
        P(("wide", "narrow"), None),
        P("narrow", "wide"),
        P("wide"),
        P("narrow"),
    )
    out_specs = (
        P(("wide", "narrow"), None),
        P(("wide", "narrow"), None),
        P(("wide", "narrow")),
        P(("wide", "narrow")),
    )
    return jax.shard_map(body, mesh=mesh, in_specs=in_specs, out_specs=out_specs, check_vma=False)
```

profile of v0, /device:TPU:0, one launch (start us, length us, event | category | flops | bytes accessed | tf_op | source)
XLA Modules:
  0.0 826.8 jit_solution(1483100814059321418)
XLA Ops:
  11.2 5.2 all-to-all-start
  22.5 5.8 gather_fusion.1
  28.4 20.9 %all-gather.5.cloned.1.call-done = bf16[1024,768]{0,1:T(8,128)(2,1)} async-done(((bf16[1024,192]{0,1:T(8,128)(2,1)}), bf16[1024,768]{0,1:T(8,128)(2,1)}) %all-gather.5.cloned.1.call-update) | async-done | bytes 1572880 | tf_op jit(solution)/shard_map/all_gather | solution.py:53
  51.2 31.1 %all-gather.3.cloned.1.call-done = bf16[2048,768]{1,0:T(8,128)(2,1)} async-done(((bf16[256,768]{1,0:T(8,128)(2,1)}), bf16[2048,768]{1,0:T(8,128)(2,1)}) %all-gather.3.cloned.1.call-update) | async-done | bytes 3145744 | tf_op jit(solution)/shard_map/all_gather | solution.py:55
  85.1 5.7 subtract_multiply_fusion.2
  90.8 362.7 %while.11 = (s32[]{:T(128)}, f32[1024]{0:T(1024)S(1)}, f32[2048,1024]{1,0:T(8,128)}, f32[2048]{0:T(1024)S(1)}, f32[1024]{0:T(1024)S(1)}, /*index=5*/s32[]{:T(128)}, s32[]{:T(128)}) while((s32[]{:T(128)}, f32[1024]{0:T(1024)S(1)}, f32[2048,1024]{1,0:T(8,128)}, f32[2048]{0:T(1024)S(1)}, f32[1024]{0:T(1024)S(1)}, ...), condition=%wide.region_13.14_spmd.clone, body=%wide.region_4.13_spmd.clone.sunk | while | flops 29370372 | bytes 33722456 | solution.py:70
  95.1 13.3 %pmax.18 = f32[2048]{0:T(1024)S(1)} all-reduce(f32[2048]{0:T(1024)S(1)} %fusion.63), channel_id=1, replica_groups=mesh['wide'=4,'narrow'=8] {'narrow'}, use_global_device_ids=true, to_apply=%region_6.0 | all-reduce | flops 2048 | bytes 16384 | tf_op jit(solution)/shard_map/while/body/eval_jaxpr/pmax | solution.py:26
  112.9 12.0 %psum.18 = f32[2048]{0:T(1024)S(1)} all-reduce(f32[2048]{0:T(1024)S(1)} %exponential_reduce_fusion.10), channel_id=1, replica_groups=mesh['wide'=4,'narrow'=8] {'narrow'}, use_global_device_ids=true, to_apply=%region_8.0 | all-reduce | flops 2048 | bytes 16384 | tf_op jit(solution)/shard_map/while/body/eval_jaxpr/psum | solution.py:27
  128.9 11.7 %pmax.19 = f32[1024]{0:T(1024)S(1)} all-reduce(f32[1024]{0:T(1024)S(1)} %fusion.64), channel_id=1, replica_groups=mesh['wide'=4,'narrow'=8] {'wide'}, use_global_device_ids=true, to_apply=%region_10.0 | all-reduce | flops 1024 | bytes 8192 | tf_op jit(solution)/shard_map/while/body/eval_jaxpr/pmax | solution.py:34
  145.0 8.4 %psum.19 = f32[1024]{0:T(1024)S(1)} all-reduce(f32[1024]{0:T(1024)S(1)} %exponential_reduce_fusion.11), channel_id=1, replica_groups=mesh['wide'=4,'narrow'=8] {'wide'}, use_global_device_ids=true, to_apply=%region_12.12 | all-reduce | flops 1024 | bytes 8192 | tf_op jit(solution)/shard_map/while/body/eval_jaxpr/psum | solution.py:35
  157.7 12.0 %pmax.18 = f32[2048]{0:T(1024)S(1)} all-reduce(f32[2048]{0:T(1024)S(1)} %fusion.63), channel_id=1, replica_groups=mesh['wide'=4,'narrow'=8] {'narrow'}, use_global_device_ids=true, to_apply=%region_6.0 | all-reduce | flops 2048 | bytes 16384 | tf_op jit(solution)/shard_map/while/body/eval_jaxpr/pmax | solution.py:26
  174.2 12.0 %psum.18 = f32[2048]{0:T(1024)S(1)} all-reduce(f32[2048]{0:T(1024)S(1)} %exponential_reduce_fusion.10), channel_id=1, replica_groups=mesh['wide'=4,'narrow'=8] {'narrow'}, use_global_device_ids=true, to_apply=%region_8.0 | all-reduce | flops 2048 | bytes 16384 | tf_op jit(solution)/shard_map/while/body/eval_jaxpr/psum | solution.py:27
  190.2 10.4 %pmax.19 = f32[1024]{0:T(1024)S(1)} all-reduce(f32[1024]{0:T(1024)S(1)} %fusion.64), channel_id=1, replica_groups=mesh['wide'=4,'narrow'=8] {'wide'}, use_global_device_ids=true, to_apply=%region_10.0 | all-reduce | flops 1024 | bytes 8192 | tf_op jit(solution)/shard_map/while/body/eval_jaxpr/pmax | solution.py:34
  205.0 8.4 %psum.19 = f32[1024]{0:T(1024)S(1)} all-reduce(f32[1024]{0:T(1024)S(1)} %exponential_reduce_fusion.11), channel_id=1, replica_groups=mesh['wide'=4,'narrow'=8] {'wide'}, use_global_device_ids=true, to_apply=%region_12.12 | all-reduce | flops 1024 | bytes 8192 | tf_op jit(solution)/shard_map/while/body/eval_jaxpr/psum | solution.py:35
  217.7 12.0 %pmax.18 = f32[2048]{0:T(1024)S(1)} all-reduce(f32[2048]{0:T(1024)S(1)} %fusion.63), channel_id=1, replica_groups=mesh['wide'=4,'narrow'=8] {'narrow'}, use_global_device_ids=true, to_apply=%region_6.0 | all-reduce | flops 2048 | bytes 16384 | tf_op jit(solution)/shard_map/while/body/eval_jaxpr/pmax | solution.py:26
  234.2 12.0 %psum.18 = f32[2048]{0:T(1024)S(1)} all-reduce(f32[2048]{0:T(1024)S(1)} %exponential_reduce_fusion.10), channel_id=1, replica_groups=mesh['wide'=4,'narrow'=8] {'narrow'}, use_global_device_ids=true, to_apply=%region_8.0 | all-reduce | flops 2048 | bytes 16384 | tf_op jit(solution)/shard_map/while/body/eval_jaxpr/psum | solution.py:27
  250.2 10.4 %pmax.19 = f32[1024]{0:T(1024)S(1)} all-reduce(f32[1024]{0:T(1024)S(1)} %fusion.64), channel_id=1, replica_groups=mesh['wide'=4,'narrow'=8] {'wide'}, use_global_device_ids=true, to_apply=%region_10.0 | all-reduce | flops 1024 | bytes 8192 | tf_op jit(solution)/shard_map/while/body/eval_jaxpr/pmax | solution.py:34
  265.0 8.4 %psum.19 = f32[1024]{0:T(1024)S(1)} all-reduce(f32[1024]{0:T(1024)S(1)} %exponential_reduce_fusion.11), channel_id=1, replica_groups=mesh['wide'=4,'narrow'=8] {'wide'}, use_global_device_ids=true, to_apply=%region_12.12 | all-reduce | flops 1024 | bytes 8192 | tf_op jit(solution)/shard_map/while/body/eval_jaxpr/psum | solution.py:35
  277.7 12.0 %pmax.18 = f32[2048]{0:T(1024)S(1)} all-reduce(f32[2048]{0:T(1024)S(1)} %fusion.63), channel_id=1, replica_groups=mesh['wide'=4,'narrow'=8] {'narrow'}, use_global_device_ids=true, to_apply=%region_6.0 | all-reduce | flops 2048 | bytes 16384 | tf_op jit(solution)/shard_map/while/body/eval_jaxpr/pmax | solution.py:26
  294.2 12.0 %psum.18 = f32[2048]{0:T(1024)S(1)} all-reduce(f32[2048]{0:T(1024)S(1)} %exponential_reduce_fusion.10), channel_id=1, replica_groups=mesh['wide'=4,'narrow'=8] {'narrow'}, use_global_device_ids=true, to_apply=%region_8.0 | all-reduce | flops 2048 | bytes 16384 | tf_op jit(solution)/shard_map/while/body/eval_jaxpr/psum | solution.py:27
  310.2 10.4 %pmax.19 = f32[1024]{0:T(1024)S(1)} all-reduce(f32[1024]{0:T(1024)S(1)} %fusion.64), channel_id=1, replica_groups=mesh['wide'=4,'narrow'=8] {'wide'}, use_global_device_ids=true, to_apply=%region_10.0 | all-reduce | flops 1024 | bytes 8192 | tf_op jit(solution)/shard_map/while/body/eval_jaxpr/pmax | solution.py:34
  325.0 8.4 %psum.19 = f32[1024]{0:T(1024)S(1)} all-reduce(f32[1024]{0:T(1024)S(1)} %exponential_reduce_fusion.11), channel_id=1, replica_groups=mesh['wide'=4,'narrow'=8] {'wide'}, use_global_device_ids=true, to_apply=%region_12.12 | all-reduce | flops 1024 | bytes 8192 | tf_op jit(solution)/shard_map/while/body/eval_jaxpr/psum | solution.py:35
  337.7 12.1 %pmax.18 = f32[2048]{0:T(1024)S(1)} all-reduce(f32[2048]{0:T(1024)S(1)} %fusion.63), channel_id=1, replica_groups=mesh['wide'=4,'narrow'=8] {'narrow'}, use_global_device_ids=true, to_apply=%region_6.0 | all-reduce | flops 2048 | bytes 16384 | tf_op jit(solution)/shard_map/while/body/eval_jaxpr/pmax | solution.py:26
  354.2 12.1 %psum.18 = f32[2048]{0:T(1024)S(1)} all-reduce(f32[2048]{0:T(1024)S(1)} %exponential_reduce_fusion.10), channel_id=1, replica_groups=mesh['wide'=4,'narrow'=8] {'narrow'}, use_global_device_ids=true, to_apply=%region_8.0 | all-reduce | flops 2048 | bytes 16384 | tf_op jit(solution)/shard_map/while/body/eval_jaxpr/psum | solution.py:27
  370.3 10.4 %pmax.19 = f32[1024]{0:T(1024)S(1)} all-reduce(f32[1024]{0:T(1024)S(1)} %fusion.64), channel_id=1, replica_groups=mesh['wide'=4,'narrow'=8] {'wide'}, use_global_device_ids=true, to_apply=%region_10.0 | all-reduce | flops 1024 | bytes 8192 | tf_op jit(solution)/shard_map/while/body/eval_jaxpr/pmax | solution.py:34
  385.1 8.4 %psum.19 = f32[1024]{0:T(1024)S(1)} all-reduce(f32[1024]{0:T(1024)S(1)} %exponential_reduce_fusion.11), channel_id=1, replica_groups=mesh['wide'=4,'narrow'=8] {'wide'}, use_global_device_ids=true, to_apply=%region_12.12 | all-reduce | flops 1024 | bytes 8192 | tf_op jit(solution)/shard_map/while/body/eval_jaxpr/psum | solution.py:35
  397.7 12.1 %pmax.18 = f32[2048]{0:T(1024)S(1)} all-reduce(f32[2048]{0:T(1024)S(1)} %fusion.63), channel_id=1, replica_groups=mesh['wide'=4,'narrow'=8] {'narrow'}, use_global_device_ids=true, to_apply=%region_6.0 | all-reduce | flops 2048 | bytes 16384 | tf_op jit(solution)/shard_map/while/body/eval_jaxpr/pmax | solution.py:26
  414.3 12.1 %psum.18 = f32[2048]{0:T(1024)S(1)} all-reduce(f32[2048]{0:T(1024)S(1)} %exponential_reduce_fusion.10), channel_id=1, replica_groups=mesh['wide'=4,'narrow'=8] {'narrow'}, use_global_device_ids=true, to_apply=%region_8.0 | all-reduce | flops 2048 | bytes 16384 | tf_op jit(solution)/shard_map/while/body/eval_jaxpr/psum | solution.py:27
  430.4 10.4 %pmax.19 = f32[1024]{0:T(1024)S(1)} all-reduce(f32[1024]{0:T(1024)S(1)} %fusion.64), channel_id=1, replica_groups=mesh['wide'=4,'narrow'=8] {'wide'}, use_global_device_ids=true, to_apply=%region_10.0 | all-reduce | flops 1024 | bytes 8192 | tf_op jit(solution)/shard_map/while/body/eval_jaxpr/pmax | solution.py:34
  445.2 8.4 %psum.19 = f32[1024]{0:T(1024)S(1)} all-reduce(f32[1024]{0:T(1024)S(1)} %exponential_reduce_fusion.11), channel_id=1, replica_groups=mesh['wide'=4,'narrow'=8] {'wide'}, use_global_device_ids=true, to_apply=%region_12.12 | all-reduce | flops 1024 | bytes 8192 | tf_op jit(solution)/shard_map/while/body/eval_jaxpr/psum | solution.py:35
  453.6 9.9 %all_gather.11 = f32[8192]{0:T(1024)S(1)} all-gather(f32[1024]{0:T(1024)S(1)} %get-tuple-element.33), channel_id=1, replica_groups=mesh['wide'=4,'narrow'=8] {'narrow'}, dimensions={0}, use_global_device_ids=true | all-gather | bytes 36864 | tf_op jit(solution)/shard_map/all_gather | solution.py:73
  463.4 6.1 gather_fusion
  474.3 7.3 select_select_fusion
  481.5 5.2 all-to-all-start.2
  488.0 87.1 %all-to-all-done.2 = bf16[8,5,128,768]{3,2,1,0:T(8,128)(2,1)} async-done(((bf16[8,5,128,768]{3,2,1,0:T(8,128)(2,1)}), bf16[8,5,128,768]{3,2,1,0:T(8,128)(2,1)}, u32[]{:S(2)}, u32[]{:S(2)}) %all-to-all-start.2) | async-done | bytes 7864352 | tf_op jit(solution)/shard_map/all_to_all | solution.py:106
  575.1 6.8 gather_fusion.2
  581.9 4.7 multiply_reduce_fusion
  604.5 4.6 all-to-all-done.4
  609.9 7.2 all_to_all.74
  635.4 4.6 all-to-all-done.7
  640.8 7.2 all_to_all.75
  666.3 4.6 all-to-all-done.10
  671.8 7.2 all_to_all.76
  695.3 20.1 %scatter_fusion = bf16[40,128,768]{2,1,0:T(8,128)(2,1)} fusion(bf16[40,128,768]{2,1,0:T(8,128)(2,1)} %broadcast_in_dim.228, s32[32]{0:T(128)S(1)} %fusion.48, bf16[32,128,768]{2,1,0:T(8,128)(2,1)} %bitcast.96), kind=kCustom, calls=%fused_computation.18 | custom fusion | bytes 18874496 | tf_op jit(solution)/shard_map/scatter | solution.py:101
  715.4 4.9 all-to-all-start.12
  720.5 5.2 fusion.7
  725.9 82.9 %all-to-all-done.12 = bf16[8,5,128,768]{3,2,1,0:T(8,128)(2,1)} async-done(((bf16[8,5,128,768]{3,2,1,0:T(8,128)(2,1)}), bf16[8,5,128,768]{3,2,1,0:T(8,128)(2,1)}, u32[]{:S(2)}, u32[]{:S(2)}) %all-to-all-start.12) | async-done | bytes 7864352 | tf_op jit(solution)/shard_map/all_to_all | solution.py:204
  808.8 9.7 %divide_convert_fusion = bf16[8,128,768]{2,0,1:T(8,128)(2,1)S(1)} fusion(f32[8,128]{0,1:T(8,128)S(1)} %fusion.41, s32[40]{0:T(128)S(1)} %reshape.452, bf16[5,8,128,768]{3,2,1,0:T(8,128)(2,1)} %bitcast.46), kind=kOutput, calls=%fused_computation.42 | convolution fusion | flops 64487744 | bytes 9441440 | tf_op jit(solution)/shard_map/dot_general | solution.py:210
  (194 shorter events, 197.6 us)
Async XLA Ops:
  7.2 15.4 %copy-start = (bf16[1024,768]{1,0:T(8,128)(2,1)S(1)}, bf16[1024,768]{1,0:T(8,128)(2,1)}, u32[]{:S(2)}) copy-start(bf16[1024,768]{1,0:T(8,128)(2,1)} %param.15) | copy-start | bytes 4718596
  7.2 42.2 %all-gather.5.cloned.1.call-start = ((), (), s32[]{:S(2)}) async-start(), calls=%async_computation.15 | async-start | bytes 1966080 | tf_op jit(solution)/shard_map/all_gather | solution.py:53
  7.9 74.4 %all-gather.3.cloned.1.call-start = ((), (), s32[]{:S(2)}) async-start(), calls=%async_computation.14 | async-start | bytes 3538944 | tf_op jit(solution)/shard_map/all_gather | solution.py:55
  11.2 9.8 %all-to-all-start = ((s32[8,1,5]{2,1,0:T(1,128)}), s32[8,1,5]{2,1,0:T(1,128)S(1)}, u32[]{:S(2)}, u32[]{:S(2)}) async-start(s32[8,1,5]{2,1,0:T(1,128)} %bitcast.2), calls=%async_computation | async-start | bytes 8192 | tf_op jit(solution)/shard_map/all_to_all | solution.py:103
  49.3 35.7 %copy-start.9 = (bf16[1024,768]{0,1:T(8,128)(2,1)S(1)}, bf16[1024,768]{0,1:T(8,128)(2,1)}, u32[]{:S(2)}) copy-start(bf16[1024,768]{0,1:T(8,128)(2,1)} %all-gather.5.cloned.1.call-done) | copy-start | bytes 4718596
  82.3 2.8 copy-start.8
  463.4 6.2 copy-start.11
  470.9 10.6 %all-to-all-start.1 = ((f32[8,5,128]{2,1,0:T(8,128)}), f32[8,5,128]{2,1,0:T(8,128)S(1)}, u32[]{:S(2)}, u32[]{:S(2)}) async-start(f32[8,5,128]{2,1,0:T(8,128)} %reshape.453), calls=%async_computation.1 | async-start | bytes 65536 | tf_op jit(solution)/shard_map/all_to_all | solution.py:136
  481.5 5.4 copy-start.7
  481.5 93.6 %all-to-all-start.2 = ((bf16[8,5,128,768]{3,2,1,0:T(8,128)(2,1)}), bf16[8,5,128,768]{3,2,1,0:T(8,128)(2,1)}, u32[]{:S(2)}, u32[]{:S(2)}) async-start(bf16[8,5,128,768]{3,2,1,0:T(8,128)(2,1)} %select_select_fusion), calls=%async_computation.2 | async-start | bytes 15728640 | tf_op jit(solution)/shard_map/all_to_all | solution.py:106
  581.9 4.7 copy-start.5
  590.1 1.4 copy-start.2
  592.8 8.1 all-to-all-start.3
  601.0 8.1 all-to-all-start.4
  617.8 4.1 copy-start.3
  623.8 8.1 all-to-all-start.6
  631.9 8.1 all-to-all-start.7
  648.7 4.1 copy-start.4
  652.8 26.9 %copy-start.10 = (f32[8,128]{1,0:T(8,128)}, f32[8,128]{1,0:T(8,128)S(1)}, u32[]{:S(2)}) copy-start(f32[8,128]{1,0:T(8,128)S(1)} %add_multiply_fusion.1) | copy-start | bytes 12292
  654.7 8.1 all-to-all-start.9
  662.9 8.1 all-to-all-start.10
  671.1 20.1 %copy-start.6 = (f32[8,128]{1,0:T(8,128)}, f32[8,128]{1,0:T(8,128)S(1)}, u32[]{:S(2)}) copy-start(f32[8,128]{1,0:T(8,128)S(1)} %add_multiply_fusion) | copy-start | bytes 12292
  683.5 31.9 %all-to-all-start.13 = ((bf16[8,5,128]{2,1,0:T(8,128)(2,1)}), bf16[8,5,128]{2,1,0:T(8,128)(2,1)S(1)}, u32[]{:S(2)}, u32[]{:S(2)}) async-start(bf16[8,5,128]{2,1,0:T(8,128)(2,1)} %reshape.480), calls=%async_computation.13 | async-start | bytes 32768 | tf_op jit(solution)/shard_map/all_to_all | solution.py:205
  715.4 93.3 %all-to-all-start.12 = ((bf16[8,5,128,768]{3,2,1,0:T(8,128)(2,1)}), bf16[8,5,128,768]{3,2,1,0:T(8,128)(2,1)}, u32[]{:S(2)}, u32[]{:S(2)}) async-start(bf16[8,5,128,768]{3,2,1,0:T(8,128)(2,1)} %bitcast.92), calls=%async_computation.12 | async-start | bytes 15728640 | tf_op jit(solution)/shard_map/all_to_all | solution.py:204
  808.8 11.2 %copy-start.1 = (bf16[1024,768]{1,0:T(8,128)(2,1)S(1)}, bf16[1024,768]{1,0:T(8,128)(2,1)}, u32[]{:S(2)}) copy-start(bf16[1024,768]{1,0:T(8,128)(2,1)} %param.15) | copy-start | bytes 4718596
Sparse Core Ops, SparseCore 0:
  9.6 39.7 all-gather.4
  51.2 31.0 all-gather.2
where the time goes:
time: 829 us; the launch traced here: 827 us
  blocking collectives  292 us (35%)
  waiting for transfers between devices  243 us (29%)
  other arithmetic  145 us (17%)
  local copies, waits for them, and re-layouts  62.1 us (7%)
  starting transfers between devices  42.1 us (5%)
  matrix products  28.6 us (3%)
  between operations  14.6 us (2%)
    all_to_all x1, waiting for transfers between devices, body(): lax.all_to_all(jnp.where((asked_ids >= 0)[:, :, None, None], found, jnp.z...  87.1 us
    all_to_all x1, waiting for transfers between devices, body(): lax.all_to_all(row_slots, 'narrow', split_axis=0, concat_axis=0, tiled=True)  82.9 us
    pmax x6, blocking collectives, lateral_lse_offset(): best_rating = lax.pmax(jnp.max(rating_grid_form, axis=1), 'narrow')  73.7 us
    psum x6, blocking collectives, lateral_lse_offset(): lax.psum(jnp.sum(jnp.exp(rating_grid_form - best_rating[:, None]), axis=1...  72.4 us
    pmax x6, blocking collectives, vertical_lse_offset(): best_rating = lax.pmax(jnp.max(rating_grid_form, axis=0), 'wide')  63.6 us
    psum x6, blocking collectives, vertical_lse_offset(): lax.psum(jnp.sum(jnp.exp(rating_grid_form - best_rating[None, :]), axis=0...  50.3 us
    all_gather x1, waiting for transfers between devices, body(): fragment = lax.all_gather(centroids_src, 'narrow', axis=0, tiled=True)  31.1 us
    reduce_sum x6, other arithmetic, lateral_lse_offset(): jnp.sum(jnp.exp(rating_grid_form - best_rating[:, None]), axis=1)  26.6 us
  transfers between devices with their start and end apart: 13, of which 11 were waited for; matrix products, arithmetic and copies ran while one was open for 8% of the time, Pallas kernels for 0%

commit v1 on v0

v1 whole, which is shorter than its diff:
```python
import functools
import math

import jax
import jax.numpy as jnp
from jax import lax
from jax.experimental import pallas as pl
from jax.experimental.pallas import tpu as pltpu
from jax.sharding import PartitionSpec as P

BLK = 128
LIST = 4
ITC = 6
STEPS = 3
HEAT = 0.02
LOG2E = math.log2(math.e)
UNIT = LOG2E / HEAT
GROUP = 4
VMEM_LIMIT = 60 * 1024 * 1024
NEG = -jnp.inf
NT = (((1,), (1,)), ((), ()))


def to_narrow(index):
    return {"narrow": index}


def to_wide(index):
    return {"wide": index}


def remote(src, dst, send, recv, target):
    return pltpu.make_async_remote_copy(
        src_ref=src,
        dst_ref=dst,
        send_sem=send,
        recv_sem=recv,
        device_id=target,
        device_id_type=pl.DeviceIdType.MESH,
    )


def barrier(n, w):
    me_n = lax.axis_index("narrow")
    me_w = lax.axis_index("wide")
    sem = pltpu.get_barrier_semaphore()
    for p in range(1, n):
        pl.semaphore_signal(
            sem, inc=1, device_id=to_narrow(lax.rem(me_n + p, n)), device_id_type=pl.DeviceIdType.MESH
        )
    for p in range(1, w):
        pl.semaphore_signal(
            sem, inc=1, device_id=to_wide(lax.rem(me_w + p, w)), device_id_type=pl.DeviceIdType.MESH
        )
    pl.semaphore_wait(sem, n - 1 + w - 1)


class Gather:
    def __init__(self, n, src, slot, send, recv):
        self.n, self.half = n, n // 2
        self.me = lax.axis_index("narrow")
        self.partner = self.me + 1 - 2 * lax.rem(self.me, 2)
        self.src, self.slot, self.send, self.recv = src, slot, send, recv

    def direct(self, p):
        return remote(
            self.src,
            self.slot(self.me),
            self.send(p - 1),
            self.recv(p - 1),
            to_narrow(lax.rem(self.me + 2 * p, self.n)),
        )

    def landed(self, p):
        at = self.slot(lax.rem(self.me + self.n - 2 * p, self.n))
        return remote(
            at, at, self.send(p - 1), self.recv(p - 1), to_narrow(lax.rem(self.me + 2 * p, self.n))
        )

    def own_pair(self):
        j = self.half - 1
        return remote(self.src, self.slot(self.me), self.send(j), self.recv(j), to_narrow(self.partner))

    def passed(self, p):
        j = self.half - 1 + p
        at = self.slot(lax.rem(self.me + self.n - 2 * p, self.n))
        return remote(at, at, self.send(j), self.recv(j), to_narrow(self.partner))

    def start(self):
        for p in range(1, self.half):
            self.direct(p).start()
        self.own_pair().start()

    def forward(self):
        for p in range(1, self.half):
            self.landed(p).wait_recv()
            self.passed(p).start()

    def finish(self):
        j = self.half - 1
        at = self.slot(self.partner)
        remote(at, at, self.send(j), self.recv(j), to_narrow(self.partner)).wait_recv()
        for p in range(1, self.half):
            j = self.half - 1 + p
            at = self.slot(lax.rem(self.partner + self.n - 2 * p, self.n))
            remote(at, at, self.send(j), self.recv(j), to_narrow(self.partner)).wait_recv()
        for p in range(1, self.half):
            self.direct(p).wait_send()
        self.own_pair().wait_send()
        for p in range(1, self.half):
            self.passed(p).wait_send()


def diagonal():
    return lax.broadcasted_iota(jnp.int32, (BLK, BLK), 0) == lax.broadcasted_iota(
        jnp.int32, (BLK, BLK), 1
    )


def as_row(column, diag):
    return jnp.sum(jnp.where(diag, column, 0.0), axis=0, keepdims=True)


def coarse_kernel(
    n,
    w,
    cs_ref,
    ct_ref,
    mu_ref,
    nu_ref,
    x_ref,
    y_ref,
    pot_ref,
    xall_ref,
    yall_ref,
    frag,
    panel,
    tile,
    frep,
    frow,
    gcol,
    bsq,
    row_out,
    row_in,
    col_out,
    col_in,
    last_in,
    fs,
    fr,
    ps,
    pr,
    bs,
    br,
    rs,
    rr,
    ks,
    kr,
    ls,
    lr,
    loc,
):
    me_n = lax.axis_index("narrow")
    me_w = lax.axis_index("wide")
    rb = cs_ref.shape[1]
    cols = ct_ref.shape[0]
    rows = rb * n
    groups = rows // BLK
    features = ct_ref.shape[1] * w
    own_rows = x_ref.shape[0]
    chunks = ITC + 2
    step_rows = own_rows // chunks
    barrier(n, w)
    diag = diagonal()

    local = [
        pltpu.make_async_copy(cs_ref, frag.at[me_n], loc.at[0]),
        pltpu.make_async_copy(ct_ref, panel.at[me_w], loc.at[1]),
        pltpu.make_async_copy(y_ref, yall_ref.at[me_n], loc.at[2]),
        pltpu.make_async_copy(x_ref, xall_ref.at[me_n], loc.at[3]),
    ]
    fg = Gather(n, cs_ref, lambda i: frag.at[i], lambda j: fs.at[j], lambda j: fr.at[j])
    fg.start()
    panels = []
    for p in range(1, w):
        c = remote(ct_ref, panel.at[me_w], ps.at[p - 1], pr.at[p - 1], to_wide(lax.rem(me_w + p, w)))
        c.start()
        panels.append(c)
    for c in local:
        c.start()

    def bulk(which, c):
        src, dst = ((y_ref, yall_ref), (x_ref, xall_ref))[which]
        at = pl.ds(pl.multiple_of(c * step_rows, step_rows), step_rows)
        return Gather(
            n,
            src.at[at],
            lambda i: dst.at[i, at],
            lambda j: bs.at[which, c, j],
            lambda j: br.at[which, c, j],
        )

    fg.forward()
    for c in range(2):
        bulk(0, c).start()
        bulk(1, c).start()
    fg.finish()
    for p in range(1, w):
        at = panel.at[lax.rem(me_w + w - p, w)]
        remote(at, at, ps.at[p - 1], pr.at[p - 1], to_wide(lax.rem(me_w + p, w))).wait_recv()
    for c in panels:
        c.wait_send()
    local[0].wait()
    local[1].wait()

    unit = 2.0 * UNIT / features
    half = min(cols, 512)

    def product(i, carry):
        for c in range(cols // half):
            acc = None
            for k in range(w):
                d = lax.dot_general(
                    frag[i, k], panel[k, c * half : (c + 1) * half, :], NT, preferred_element_type=jnp.float32
                )
                acc = d if acc is None else acc + d
            tile[pl.ds(pl.multiple_of(i * rb, rb), rb), c * half : (c + 1) * half] = acc * unit
        return carry

    lax.fori_loop(0, n, product, 0)
    for g in range(cols // BLK):
        sq = jnp.zeros((BLK, 1), jnp.float32)
        for k in range(w):
            v = panel[k, g * BLK : (g + 1) * BLK, :].astype(jnp.float32)
            sq = sq + jnp.sum(v * v, axis=1, keepdims=True)
        bsq[:, g * BLK : (g + 1) * BLK] = as_row(sq, diag) * (UNIT / features)
    gcol[...] = -bsq[...]
    sub = 32
    cg = cols // BLK

    def turn(it, carry):
        g_now = gcol[...]

        def row_group(g, c2):
            ms, zs = [], []
            for s in range(BLK // sub):
                start = pl.multiple_of(g * BLK + s * sub, sub)
                t = tile[pl.ds(start, sub), :] + g_now
                m = jnp.max(t, axis=1, keepdims=True)
                z = jnp.sum(jnp.exp2(t - m), axis=1, keepdims=True)
                ms.append(m)
                zs.append(z)
            row_out[it, pl.ds(g, 1), :] = as_row(jnp.concatenate(ms, axis=0), diag)
            row_out[it, pl.ds(groups + g, 1), :] = as_row(jnp.concatenate(zs, axis=0), diag)
            return c2

        lax.fori_loop(0, groups, row_group, 0)
        sent = []
        for p in range(1, n):
            c = remote(
                row_out.at[it],
                row_in.at[it, p - 1],
                rs.at[it, p - 1],
                rr.at[it, p - 1],
                to_narrow(lax.rem(me_n + p, n)),
            )
            c.start()
            sent.append(c)
        bulk(0, it + 2).start()
        for c in sent:
            c.wait_recv()
        top = row_out[it, 0:groups, :]
        for p in range(n - 1):
            top = jnp.maximum(top, row_in[it, p, 0:groups, :])
        total = row_out[it, groups : 2 * groups, :] * jnp.exp2(row_out[it, 0:groups, :] - top)
        for p in range(n - 1):
            total = total + row_in[it, p, groups : 2 * groups, :] * jnp.exp2(
                row_in[it, p, 0:groups, :] - top
            )
        frow[...] = jnp.log2(mu_ref[...]) - (top + jnp.log2(total))
        bulk(0, it).forward()

        def spread(g, c2):
            line = jnp.broadcast_to(frow[pl.ds(g, 1), :], (BLK, BLK))
            frep[pl.ds(pl.multiple_of(g * BLK, BLK), BLK), :] = line.T
            return c2

        lax.fori_loop(0, groups, spread, 0)
        span = 64

        def top_step(r, tops):
            start = pl.multiple_of(r * span, span)
            f = frep[pl.ds(start, span), :]
            out = []
            for c in range(cg):
                t = f + tile[pl.ds(start, span), c * BLK : (c + 1) * BLK]
                out.append(jnp.maximum(tops[c], jnp.max(t.reshape(span // 8, 8, BLK), axis=0)))
            return tuple(out)

        tops = lax.fori_loop(
            0, rows // span, top_step, tuple(jnp.full((8, BLK), NEG, jnp.float32) for _ in range(cg))
        )
        tops = tuple(jnp.broadcast_to(jnp.max(t, axis=0, keepdims=True), (8, BLK)) for t in tops)

        def sum_step(r, sums):
            start = pl.multiple_of(r * span, span)
            f = frep[pl.ds(start, span), :]
            out = []
            for c in range(cg):
                t = (f + tile[pl.ds(start, span), c * BLK : (c + 1) * BLK]).reshape(span // 8, 8, BLK)
                out.append(sums[c] + jnp.sum(jnp.exp2(t - tops[c][None]), axis=0))
            return tuple(out)

        sums = lax.fori_loop(
            0, rows // span, sum_step, tuple(jnp.zeros((8, BLK), jnp.float32) for _ in range(cg))
        )
        for c in range(cg):
            col_out[it, 0:1, c * BLK : (c + 1) * BLK] = tops[c][0:1]
            col_out[it, 1:2, c * BLK : (c + 1) * BLK] = jnp.sum(sums[c], axis=0, keepdims=True)
        csent = []
        for p in range(1, w):
            c = remote(
                col_out.at[it],
                col_in.at[it, p - 1],
                ks.at[it, p - 1],
                kr.at[it, p - 1],
                to_wide(lax.rem(me_w + p, w)),
            )
            c.start()
            csent.append(c)
        bulk(1, it + 2).start()
        for c in csent:
            c.wait_recv()
        top = col_out[it, 0:1, :]
        for p in range(w - 1):
            top = jnp.maximum(top, col_in[it, p, 0:1, :])
        total = col_out[it, 1:2, :] * jnp.exp2(col_out[it, 0:1, :] - top)
        for p in range(w - 1):
            total = total + col_in[it, p, 1:2, :] * jnp.exp2(col_in[it, p, 0:1, :] - top)
        gcol[...] = jnp.log2(nu_ref[...]) - (top + jnp.log2(total))
        bulk(1, it).forward()
        for c in sent:
            c.wait_send()
        for c in csent:
            c.wait_send()
        return carry

    lax.fori_loop(0, ITC, turn, 0)
    gcol[...] = gcol[...] + bsq[...]
    last = []
    for p in range(1, n):
        c = remote(
            gcol, last_in.at[p - 1], ls.at[p - 1], lr.at[p - 1], to_narrow(lax.rem(me_n + p, n))
        )
        c.start()
        last.append(c)
    pot_ref[me_n] = gcol[...]
    for c in last:
        c.wait_recv()
    for p in range(1, n):
        pot_ref[lax.rem(me_n + n - p, n)] = last_in[p - 1]
    for c in last:
        c.wait_send()
    for c in range(ITC, chunks):
        bulk(0, c).forward()
        bulk(1, c).forward()

    def close(c, carry):
        bulk(0, c).finish()
        bulk(1, c).finish()
        return carry

    lax.fori_loop(0, chunks, close, 0)
    local[2].wait()
    local[3].wait()


def coarse_call(n, w, cs, ct, mu, nu, x, y):
    rb = cs.shape[1]
    cols, part = ct.shape
    rows = rb * n
    groups = rows // BLK
    chunks = ITC + 2
    dma = pltpu.SemaphoreType.DMA
    vm = pl.BlockSpec(memory_space=pltpu.VMEM)
    anyspace = pl.BlockSpec(memory_space=pl.ANY)
    f32 = jnp.float32
    return pl.pallas_call(
        functools.partial(coarse_kernel, n, w),
        out_shape=(
            jax.ShapeDtypeStruct((n, 1, cols), f32),
            jax.ShapeDtypeStruct((n,) + x.shape, x.dtype),
            jax.ShapeDtypeStruct((n,) + y.shape, y.dtype),
        ),
        in_specs=[vm] * 6,
        out_specs=(vm, anyspace, anyspace),
        scratch_shapes=[
            pltpu.VMEM((n, w, rb, part), cs.dtype),
            pltpu.VMEM((w, cols, part), ct.dtype),
            pltpu.VMEM((rows, cols), f32),
            pltpu.VMEM((rows, BLK), f32),
            pltpu.VMEM((groups, BLK), f32),
            pltpu.VMEM((1, cols), f32),
            pltpu.VMEM((1, cols), f32),
            pltpu.VMEM((ITC, 2 * groups, BLK), f32),
            pltpu.VMEM((ITC, n - 1, 2 * groups, BLK), f32),
            pltpu.VMEM((ITC, 2, cols), f32),
            pltpu.VMEM((ITC, w - 1, 2, cols), f32),
            pltpu.VMEM((n - 1, 1, cols), f32),
            dma((n - 1,)),
            dma((n - 1,)),
            dma((w - 1,)),
            dma((w - 1,)),
            dma((2, chunks, n - 1)),
            dma((2, chunks, n - 1)),
            dma((ITC, n - 1)),
            dma((ITC, n - 1)),
            dma((ITC, w - 1)),
            dma((ITC, w - 1)),
            dma((n - 1,)),
            dma((n - 1,)),
            dma((4,)),
        ],
        compiler_params=pltpu.CompilerParams(
            collective_id=0, has_side_effects=True, vmem_limit_bytes=VMEM_LIMIT
        ),
        name="coarse",
    )(cs, ct, mu, nu, x, y)


def score_kernel(unit, row_pick, index_ref, own_ref, *refs):
    out = refs[-1]
    step = pl.program_id(0)
    for l in range(GROUP):
        left = own_ref[row_pick(index_ref, step, l)]
        out[l] = lax.dot_general(left, refs[l][0], NT, preferred_element_type=jnp.float32) * unit


def score_call(unit, row_pick, meta, own, pool, entries):
    feature_count = own.shape[-1]

    def pick(l):
        return lambda i, meta_ref: (meta_ref[0, i * GROUP + l], 0, 0)

    return pl.pallas_call(
        functools.partial(score_kernel, unit, row_pick),
        out_shape=jax.ShapeDtypeStruct((entries, BLK, BLK), jnp.float32),
        grid_spec=pltpu.PrefetchScalarGridSpec(
            num_scalar_prefetch=1,
            grid=(entries // GROUP,),
            in_specs=[pl.BlockSpec(own.shape, lambda i, m: (0, 0, 0))]
            + [pl.BlockSpec((1, BLK, feature_count), pick(l)) for l in range(GROUP)],
            out_specs=pl.BlockSpec((GROUP, BLK, BLK), lambda i, m: (i, 0, 0)),
        ),
        compiler_params=pltpu.CompilerParams(vmem_limit_bytes=VMEM_LIMIT),
        name="scores",
    )(meta, own, *([pool] * GROUP))


def fine_kernel(
    n,
    w,
    smeta,
    tmeta,
    ms_ref,
    mt_ref,
    live_ref,
    coarse_ref,
    cl_ref,
    asq_ref,
    bsq_ref,
    fpot_ref,
    gpot_ref,
    ps_ref,
    pt_ref,
    *scratch,
):
    pots = scratch[: 2 * STEPS + 1]
    own_g, mbuf, zbuf, send, recv = scratch[2 * STEPS + 1 :]
    me_n = lax.axis_index("narrow")
    sb = asq_ref.shape[0]
    tb = bsq_ref.shape[0]
    slots = mt_ref.shape[0]
    barrier(n, w)
    diag = diagonal()

    def region(i, count):
        return pl.ds(pl.multiple_of(i * count, count), count)

    def share(x, count):
        for p in range(1, n):
            at = pots[x].at[region(me_n, count)]
            remote(
                at, at, send.at[x, p - 1], recv.at[x, p - 1], to_narrow(lax.rem(me_n + p, n))
            ).start()

    def arrive(x, count):
        for p in range(1, n):
            at = pots[x].at[region(lax.rem(me_n + n - p, n), count)]
            remote(
                at, at, send.at[x, p - 1], recv.at[x, p - 1], to_narrow(lax.rem(me_n + p, n))
            ).wait_recv()
        for p in range(1, n):
            at = pots[x].at[region(me_n, count)]
            remote(
                at, at, send.at[x, p - 1], recv.at[x, p - 1], to_narrow(lax.rem(me_n + p, n))
            ).wait_send()

    points = cl_ref.shape[1]
    hi = coarse_ref.shape[1]
    clusters = cl_ref[...]
    spread = jnp.where(
        lax.broadcasted_iota(jnp.int32, (hi, points), 0) == clusters // BLK, 1.0, 0.0
    ).astype(jnp.float32)
    picked = jnp.dot(
        coarse_ref[...], spread, preferred_element_type=jnp.float32, precision=lax.Precision.HIGHEST
    )
    lane = lax.broadcasted_iota(jnp.int32, (BLK, points), 0) == lax.rem(clusters, BLK)
    begin = jnp.sum(jnp.where(lane, picked, 0.0), axis=0, keepdims=True)
    for b in range(tb):
        pots[0][pl.ds(me_n * tb + b, 1), :] = (
            begin[:, b * BLK : (b + 1) * BLK] - bsq_ref[b : b + 1, :]
        )
    share(0, tb)

    for k in range(STEPS):
        gx = 2 * k
        fx = 2 * k + 1
        nx = 2 * k + 2
        arrive(gx, tb)

        def src_block(b, c2, gx=gx, fx=fx):
            ts = []
            top = None
            for l in range(LIST):
                e = b * LIST + l
                t = ms_ref[e] + pots[gx][pl.ds(smeta[e], 1), :]
                ts.append(t)
                top = t if top is None else jnp.maximum(top, t)
            top = jnp.max(top, axis=1, keepdims=True)
            total = None
            for t in ts:
                v = jnp.exp2(t - top)
                total = v if total is None else total + v
            total = jnp.sum(total, axis=1, keepdims=True)
            pots[fx][pl.ds(me_n * sb + b, 1), :] = as_row(-(top + jnp.log2(total)), diag)
            return c2

        lax.fori_loop(0, sb, src_block, 0)
        share(fx, sb)
        arrive(fx, sb)

        def slot_step(s, c2, fx=fx):
            for u in range(2):
                e = s * 2 + u
                t = mt_ref[e] + pots[fx][pl.ds(tmeta[0, e], 1), :]
                top = jnp.max(t, axis=1, keepdims=True)
                total = jnp.sum(jnp.exp2(t - top), axis=1, keepdims=True)
                mbuf[pl.ds(e, 1), :] = as_row(top, diag)
                zbuf[pl.ds(e, 1), :] = as_row(total, diag)
            return c2

        lax.fori_loop(0, slots // 2, slot_step, 0)
        live = live_ref[...]
        m_all = mbuf[...]
        z_all = zbuf[...]
        for b in range(tb):
            mask = live == b
            top = jnp.max(jnp.where(mask, m_all, NEG), axis=0, keepdims=True)
            part = z_all * jnp.exp2(jnp.where(mask, m_all - top, 0.0))
            total = jnp.sum(jnp.where(mask, part, 0.0), axis=0, keepdims=True)
            line = -(top + jnp.log2(total))
            pots[nx][pl.ds(me_n * tb + b, 1), :] = line
            own_g[b : b + 1, :] = line
        share(nx, tb)

    fx, gx = 2 * STEPS - 1, 2 * STEPS

    def target_plan(s, c2):
        g_line = own_g[pl.ds(tmeta[1, s], 1), :]
        g_col = jnp.broadcast_to(g_line, (BLK, BLK)).T
        t = mt_ref[s] + pots[fx][pl.ds(tmeta[0, s], 1), :] + g_col
        alive = live_ref[pl.ds(s, 1), :] >= 0
        pt_ref[s] = jnp.where(alive, jnp.exp2(t), 0.0).astype(jnp.bfloat16)
        return c2

    lax.fori_loop(0, slots, target_plan, 0)
    fpot_ref[...] = (pots[fx][region(me_n, sb), :] + asq_ref[...]) * (1.0 / UNIT)
    gpot_ref[...] = (own_g[...] + bsq_ref[...]) * (1.0 / UNIT)
    arrive(gx, tb)

    def source_plan(b, c2):
        f_line = pots[fx][pl.ds(me_n * sb + b, 1), :]
        f_col = jnp.broadcast_to(f_line, (BLK, BLK)).T
        for l in range(LIST):
            e = b * LIST + l
            t = ms_ref[e] + pots[gx][pl.ds(smeta[e], 1), :] + f_col
            ps_ref[e] = jnp.exp2(t).astype(jnp.bfloat16)
        return c2

    lax.fori_loop(0, sb, source_plan, 0)


def fine_call(n, w, smeta, tmeta, ms, mt, live, coarse, clusters, asq, bsq):
    vm = pl.BlockSpec(memory_space=pltpu.VMEM)
    sm = pl.BlockSpec(memory_space=pltpu.SMEM)
    dma = pltpu.SemaphoreType.DMA
    f32 = jnp.float32
    turns = 2 * STEPS + 1
    held = n * max(asq.shape[0], bsq.shape[0])
    slots = mt.shape[0]
    return pl.pallas_call(
        functools.partial(fine_kernel, n, w),
        out_shape=(
            jax.ShapeDtypeStruct(asq.shape, f32),
            jax.ShapeDtypeStruct(bsq.shape, f32),
            jax.ShapeDtypeStruct(ms.shape, jnp.bfloat16),
            jax.ShapeDtypeStruct(mt.shape, jnp.bfloat16),
        ),
        in_specs=[sm, sm] + [vm] * 7,
        out_specs=(vm,) * 4,
        scratch_shapes=[
            *[pltpu.VMEM((held, BLK), f32) for _ in range(turns)],
            pltpu.VMEM(bsq.shape, f32),
            pltpu.VMEM((slots, BLK), f32),
            pltpu.VMEM((slots, BLK), f32),
            dma((turns, n - 1)),
            dma((turns, n - 1)),
        ],
        compiler_params=pltpu.CompilerParams(
            collective_id=1, has_side_effects=True, vmem_limit_bytes=VMEM_LIMIT
        ),
        name="fine",
    )(smeta, tmeta, ms, mt, live, coarse, clusters, asq, bsq)


def source_mean_kernel(meta, plan_ref, *refs):
    out = refs[-1]
    num = None
    den = None
    for l in range(LIST):
        p = plan_ref[l]
        d = jnp.dot(p, refs[l][0], preferred_element_type=jnp.float32)
        s = p.astype(jnp.float32)
        num = d if num is None else num + d
        den = s if den is None else den + s
    out[...] = (num / jnp.sum(den, axis=1, keepdims=True)).astype(out.dtype)


def source_mean(meta, plan, pool):
    entries = plan.shape[0]
    feature_count = pool.shape[-1]

    def pick(l):
        return lambda i, m: (m[0, i * LIST + l], 0, 0)

    return pl.pallas_call(
        source_mean_kernel,
        out_shape=jax.ShapeDtypeStruct((entries // LIST * BLK, feature_count), pool.dtype),
        grid_spec=pltpu.PrefetchScalarGridSpec(
            num_scalar_prefetch=1,
            grid=(entries // LIST,),
            in_specs=[pl.BlockSpec((LIST, BLK, BLK), lambda i, m: (i, 0, 0))]
            + [pl.BlockSpec((1, BLK, feature_count), pick(l)) for l in range(LIST)],
            out_specs=pl.BlockSpec((BLK, feature_count), lambda i, m: (i, 0)),
        ),
        compiler_params=pltpu.CompilerParams(vmem_limit_bytes=VMEM_LIMIT),
        name="source_mean",
    )(meta, plan, *([pool] * LIST))


def target_mean_kernel(tb, meta, plan_ref, *refs):
    blocks, (out, num, den) = refs[:GROUP], refs[GROUP:]
    step = pl.program_id(0)

    @pl.when(step == 0)
    def _():
        num[...] = jnp.zeros_like(num)
        den[...] = jnp.zeros_like(den)

    for l in range(GROUP):
        t = meta[1, step * GROUP + l]
        p = plan_ref[l]
        num[t] += jnp.dot(p, blocks[l][0], preferred_element_type=jnp.float32)
        den[t] += p.astype(jnp.float32)

    @pl.when(step == pl.num_programs(0) - 1)
    def _():
        def write(t, carry):
            total = jnp.sum(den[t], axis=1, keepdims=True)
            out[pl.ds(pl.multiple_of(t * BLK, BLK), BLK), :] = (num[t] / total).astype(out.dtype)
            return carry

        lax.fori_loop(0, tb, write, 0)


def target_mean(tb, meta, plan, pool):
    slots = plan.shape[0]
    feature_count = pool.shape[-1]

    def pick(l):
        return lambda i, m: (m[0, i * GROUP + l], 0, 0)

    return pl.pallas_call(
        functools.partial(target_mean_kernel, tb),
        out_shape=jax.ShapeDtypeStruct((tb * BLK, feature_count), pool.dtype),
        grid_spec=pltpu.PrefetchScalarGridSpec(
            num_scalar_prefetch=1,
            grid=(slots // GROUP,),
            in_specs=[pl.BlockSpec((GROUP, BLK, BLK), lambda i, m: (i, 0, 0))]
            + [pl.BlockSpec((1, BLK, feature_count), pick(l)) for l in range(GROUP)],
            out_specs=pl.BlockSpec((tb * BLK, feature_count), lambda i, m: (0, 0)),
            scratch_shapes=[
                pltpu.VMEM((tb, BLK, feature_count), jnp.float32),
                pltpu.VMEM((tb, BLK, BLK), jnp.float32),
            ],
        ),
        compiler_params=pltpu.CompilerParams(vmem_limit_bytes=VMEM_LIMIT),
        name="target_mean",
    )(meta, plan, *([pool] * GROUP))


def square_norms(rows_in):
    return jnp.sum(jnp.square(rows_in.astype(jnp.float32)), axis=-1)


def own_block_of_entry(meta_ref, step, l):
    return step


def own_block_of_slot(meta_ref, step, l):
    return meta_ref[1, step * GROUP + l]


def body(
    sources,
    targets,
    target_lists,
    target_clusters,
    centroids_src,
    centroids_tgt,
    sender_mean_measure,
    recipient_mean_measure,
):
    feature_count = sources.shape[1]
    n = lax.axis_size("narrow")
    w = lax.axis_size("wide")
    sb = sources.shape[0] // BLK
    tb = targets.shape[0] // BLK
    wanted = target_lists.reshape(-1)
    entries = wanted.shape[0]
    capacity = max(
        (5 * sb * LIST + 4 * n - 1) // (4 * n),
        (tb + n - 1) // n,
    )
    slots = n * capacity
    index = jnp.arange(entries, dtype=jnp.int32)
    owner_of = wanted // tb % n
    local_block = wanted % tb
    earlier = jnp.logical_and(owner_of[:, None] == owner_of[None, :], index[None, :] < index[:, None])
    slot_of = owner_of * capacity + jnp.sum(earlier.astype(jnp.int32), axis=1)
    code = local_block + tb * (index // LIST) + 1
    hit = slot_of[None, :] == jnp.arange(slots, dtype=jnp.int32)[:, None]
    requests = jnp.sum(jnp.where(hit, code[None, :], 0), axis=1).reshape(n, capacity)
    asked = lax.all_to_all(requests, "narrow", split_axis=0, concat_axis=0, tiled=True)
    asked = asked.reshape(-1) - 1
    alive = asked >= 0
    clipped = jnp.maximum(asked, 0)
    from_block = (jnp.arange(slots, dtype=jnp.int32) // capacity) * sb + clipped // tb
    to_block = clipped % tb
    tmeta = jnp.stack([from_block, to_block])
    live = jnp.broadcast_to(jnp.where(alive, to_block, -1)[:, None], (slots, BLK))
    smeta = owner_of * tb + local_block

    cs = centroids_src.reshape(centroids_src.shape[0], w, -1).transpose(1, 0, 2)
    mu = sender_mean_measure.reshape(-1, BLK)
    nu = recipient_mean_measure.reshape(1, -1)
    coarse, xall, yall = coarse_call(n, w, cs, centroids_tgt, mu, nu, sources, targets)
    xall = xall.reshape(n * sb, BLK, feature_count)
    yall = yall.reshape(n * tb, BLK, feature_count)
    src_blocks = sources.reshape(sb, BLK, feature_count)
    tgt_blocks = targets.reshape(tb, BLK, feature_count)
    unit = 2.0 * UNIT / feature_count
    ms = score_call(unit, own_block_of_entry, smeta[None, :], src_blocks, yall, entries)
    mt = score_call(unit, own_block_of_slot, tmeta, tgt_blocks, xall, slots)
    asq = square_norms(src_blocks) * (UNIT / feature_count)
    bsq = square_norms(tgt_blocks) * (UNIT / feature_count)
    src_potential, tgt_potential, ps, pt = fine_call(
        n,
        w,
        smeta,
        tmeta,
        ms,
        mt,
        live,
        coarse.reshape(-1, BLK).T,
        target_clusters.reshape(1, -1),
        asq,
        bsq,
    )
    src_bary = source_mean(smeta[None, :], ps, yall)
    tgt_bary = target_mean(tb, tmeta, pt, xall)
    return (src_bary, tgt_bary, src_potential.reshape(-1), tgt_potential.reshape(-1))


def solution(mesh):
    in_specs = (
        P(("wide", "narrow"), None),
        P(("wide", "narrow"), None),
        P(("wide", "narrow"), None),
        P(("wide", "narrow")),
        P(("wide", "narrow"), None),
        P("narrow", "wide"),
        P("wide"),
        P("narrow"),
    )
    out_specs = (
        P(("wide", "narrow"), None),
        P(("wide", "narrow"), None),
        P(("wide", "narrow")),
        P(("wide", "narrow")),
    )
    return jax.shard_map(body, mesh=mesh, in_specs=in_specs, out_specs=out_specs, check_vma=False)
```

time: 829 us -> 297 us (0.36)
  blocking collectives: 292 us -> 0 us
  Pallas kernels: 0 us -> 278 us
  waiting for transfers between devices: 243 us -> 0.01 us
  other arithmetic: 145 us -> 4.94 us
  local copies, waits for them, and re-layouts: 62.1 us -> 7.69 us
  starting transfers between devices: 42.1 us -> 5.2 us
  matrix products: 28.6 us -> 0 us
  between operations: 14.6 us -> 0.72 us
    pallas_call x0 -> x6, Pallas kernels: none -> 278 us  [the longest x1 187 us: coarse_call(): pl.pallas_call(functools.partial(coarse_kernel, n, w), out_shape=(jax.Sha...]
    all_to_all x10 -> x0, waiting for transfers between devices: 187 us -> none  [the longest x1 87.1 us: body(): lax.all_to_all(jnp.where((asked_ids >= 0)[:, :, None, None], found, jnp.z...]
    pmax x12 -> x0, blocking collectives: 137 us -> none  [the longest x6 73.7 us: lateral_lse_offset(): best_rating = lax.pmax(jnp.max(rating_grid_form, axis=1), 'narrow')]
    psum x12 -> x0, blocking collectives: 123 us -> none  [the longest x6 72.4 us: lateral_lse_offset(): lax.psum(jnp.sum(jnp.exp(rating_grid_form - best_rating[:, None]), axis=1...]
    reduce_sum x24 -> x2, other arithmetic: 68.3 us -> 0.27 us  [the longest x1 0.18 us: body(): slot_of = owner_of * capacity + jnp.sum(earlier.astype(jnp.int32), axis=1)]
    reduce_max x20 -> x0, other arithmetic: 55.8 us -> none  [the longest x6 25.6 us: lateral_lse_offset(): best_rating = lax.pmax(jnp.max(rating_grid_form, axis=1), 'narrow')]
    all_gather x2 -> x0, waiting for transfers between devices: 52 us -> none  [the longest x1 31.1 us: body(): fragment = lax.all_gather(centroids_src, 'narrow', axis=0, tiled=True)]
    all_to_all x10 -> x0, starting transfers between devices: 36.9 us -> none  [the longest x3 10 us: body(): lax.all_to_all(sum_slots, 'narrow', split_axis=0, concat_axis=0, tiled=True)]
  transfers between devices with their start and end apart: 13 -> 1, of which waited for: 11 -> 0; matrix products, arithmetic and copies ran while one was open for 8% -> 2% of each run, Pallas kernels for 0% -> 66%
where the time goes in v1:
time: 297 us; the launch traced here: 296 us
  Pallas kernels  278 us (94%)
  local copies, waits for them, and re-layouts  7.69 us (3%)
  starting transfers between devices  5.2 us (2%)
  other arithmetic  4.94 us (2%)
    pallas_call x1, Pallas kernels, coarse_call(): pl.pallas_call(functools.partial(coarse_kernel, n, w), out_shape=(jax.Sha...  187 us
    pallas_call x1, Pallas kernels, fine_call(): pl.pallas_call(functools.partial(fine_kernel, n, w), out_shape=(jax.Shape...  50.3 us
    pallas_call x2, Pallas kernels, score_call(): pl.pallas_call(functools.partial(score_kernel, unit, row_pick), out_shape...  20 us
    pallas_call x1, Pallas kernels, target_mean(): pl.pallas_call(functools.partial(target_mean_kernel, tb), out_shape=jax.S...  11.5 us
    pallas_call x1, Pallas kernels, source_mean(): pl.pallas_call(source_mean_kernel, out_shape=jax.ShapeDtypeStruct((entrie...  8.7 us
  transfers between devices with their start and end apart: 1, of which 0 were waited for; matrix products, arithmetic and copies ran while one was open for 2% of the time, Pallas kernels for 66%

profile of v1, /device:TPU:0, one launch (start us, length us, event | category | flops | bytes accessed | tf_op | source)
XLA Modules:
  0.0 296.2 jit_solution(10529750211974855522)
XLA Ops:
  0.6 0.0 copy-start
  0.6 0.0 copy-start.2
  0.7 0.9 copy.35
  1.5 0.1 reshape.407
  1.6 0.6 multiply_add_fusion.1
  2.2 0.2 convert_reduce_fusion
  2.4 0.1 select_reduce_fusion
  2.5 0.7 all_to_all.6
  3.2 5.2 %all-to-all-start = ((s32[8,1,5]{2,1,0:T(1,128)}), s32[8,1,5]{2,1,0:T(1,128)S(1)}, u32[]{:S(2)}, u32[]{:S(2)}) async-start(s32[8,1,5]{2,1,0:T(1,128)} %bitcast), calls=%async_computation | async-start | bytes 8192 | tf_op jit(solution)/shard_map/all_to_all | solution.py:764
  8.4 0.1 reshape.406
  8.4 0.6 fusion.1.index_ref.meta
  9.1 0.0 copy-start.1
  9.1 1.8 multiply_reduce_fusion.1
  10.9 0.0 copy-done
  10.9 0.4 multiply_reduce_fusion
  11.3 0.0 copy-done.2
  11.3 0.2 copy.38
  11.5 1.0 copy.39
  12.5 0.0 copy-done.1
  12.5 1.0 copy.40.ct_ref
  13.5 187.1 %coarse.1 = (f32[8,1,1024]{2,1,0:T(1,128)}, bf16[8,1024,768]{2,1,0:T(8,128)(2,1)}, bf16[8,1024,768]{2,1,0:T(8,128)(2,1)}) custom-call(bf16[4,256,192]{2,1,0:T(8,128)(2,1)} %bitcast.37, bf16[1024,192]{1,0:T(8,128)(2,1)} %copy.40.ct_ref, f32[16,128]{1,0:T(8,128)} %bitcast.42, f32[1,1024]{1,0:T(1,128)} %bitcast.43, bf16[1024,768]{1,0:T(8,128)(2,1)} %x_ref.1, ...), custom_call_target="tpu_custom_call" | custom-call | tf_op jit(solution)/shard_map/coarse/pallas_call | solution.py:387
  200.6 1.5 copy.41
  202.0 0.6 multiply_bitcast_fusion
  202.6 9.2 %scores.2.ms_ref = f32[32,128,128]{2,1,0:T(8,128)} custom-call(s32[1,32]{1,0:T(1,128)} %fusion.1.index_ref.meta, bf16[8,128,768]{2,1,0:T(8,128)(2,1)} %bitcast.35, bf16[64,128,768]{2,1,0:T(8,128)(2,1)} %bitcast.19, bf16[64,128,768]{2,1,0:T(8,128)(2,1)} %bitcast.20, bf16[64,128,768]{2,1,0:T(8,128)(2,1)} %bitcast.21, bf16[64,128,768]{2,1,0:T(8,128)(2,1)} %bitcast.22), custom_call_target="tpu_custom_call" | custom-call | tf_op jit(solution)/shard_map/scores/pallas_call | solution.py:444
  211.8 0.0 all-to-all-done
  211.9 0.1 ge.11
  211.9 0.1 ne.239
  212.1 0.1 div.60
  212.1 0.1 rem.142
  212.2 0.1 rem.143
  212.3 0.6 pad_add_fusion.index_ref.tmeta.meta
  212.9 10.9 %scores.3.mt_ref = f32[40,128,128]{2,1,0:T(8,128)} custom-call(s32[2,40]{1,0:T(2,128)} %pad_add_fusion.index_ref.tmeta.meta, bf16[8,128,768]{2,1,0:T(8,128)(2,1)} %bitcast.36, bf16[64,128,768]{2,1,0:T(8,128)(2,1)} %bitcast.27, bf16[64,128,768]{2,1,0:T(8,128)(2,1)} %bitcast.28, bf16[64,128,768]{2,1,0:T(8,128)(2,1)} %bitcast.29, bf16[64,128,768]{2,1,0:T(8,128)(2,1)} %bitcast.30), custom_call_target="tpu_custom_call" | custom-call | tf_op jit(solution)/shard_map/scores/pallas_call | solution.py:444
  223.8 0.7 broadcast_in_dim.18.live_ref
  224.5 50.3 %fine.1 = (f32[8,128]{1,0:T(8,128)}, f32[8,128]{1,0:T(8,128)}, bf16[32,128,128]{2,1,0:T(8,128)(2,1)}, bf16[40,128,128]{2,1,0:T(8,128)(2,1)}) custom-call(s32[32]{0:T(128)} %get-tuple-element.24.smeta, s32[2,40]{1,0:T(2,128)} %pad_add_fusion.index_ref.tmeta.meta, f32[32,128,128]{2,1,0:T(8,128)} %scores.2.ms_ref, f32[40,128,128]{2,1,0:T(8,128)} %scores.3.mt_ref, ...), custom_call_target="tpu_custom_call" | custom-call | tf_op jit(solution)/shard_map/fine/pallas_call | solution.py:611
  274.8 11.5 %target_mean.1 = bf16[1024,768]{1,0:T(8,128)(2,1)} custom-call(s32[2,40]{1,0:T(2,128)} %pad_add_fusion.index_ref.tmeta.meta, bf16[40,128,128]{2,1,0:T(8,128)(2,1)} %get-tuple-element.15.plan_ref, bf16[64,128,768]{2,1,0:T(8,128)(2,1)} %bitcast.31, bf16[64,128,768]{2,1,0:T(8,128)(2,1)} %bitcast.32, bf16[64,128,768]{2,1,0:T(8,128)(2,1)} %bitcast.33, ...), custom_call_target="tpu_custom_call" | custom-call | tf_op jit(solution)/shard_map/target_mean/pallas_call | solution.py:703
  286.3 0.0 copy-start.4
  286.3 0.0 copy-start.3
  286.3 8.7 %source_mean.1 = bf16[1024,768]{1,0:T(8,128)(2,1)} custom-call(s32[1,32]{1,0:T(1,128)} %fusion.1.index_ref.meta, bf16[32,128,128]{2,1,0:T(8,128)(2,1)} %get-tuple-element.14.plan_ref, bf16[64,128,768]{2,1,0:T(8,128)(2,1)} %bitcast.23, bf16[64,128,768]{2,1,0:T(8,128)(2,1)} %bitcast.24, bf16[64,128,768]{2,1,0:T(8,128)(2,1)} %bitcast.25, ...), custom_call_target="tpu_custom_call" | custom-call | tf_op jit(solution)/shard_map/source_mean/pallas_call | solution.py:656
  295.0 0.0 copy-done.4
  295.0 0.6 copy.44
  295.6 0.0 copy-done.3
  295.6 0.6 copy.45
  (6 shorter events, 0.1 us)
Async XLA Ops:
  0.6 10.3 %copy-start = (bf16[1024,768]{1,0:T(8,128)(2,1)S(1)}, bf16[1024,768]{1,0:T(8,128)(2,1)}, u32[]{:S(2)}) copy-start(bf16[1024,768]{1,0:T(8,128)(2,1)} %y_ref.1) | copy-start | bytes 4718596
  0.6 10.6 %copy-start.2 = (bf16[256,768]{1,0:T(8,128)(2,1)S(1)}, bf16[256,768]{1,0:T(8,128)(2,1)}, u32[]{:S(2)}) copy-start(bf16[256,768]{1,0:T(8,128)(2,1)} %param.12) | copy-start | bytes 1179652
  3.2 208.6 %all-to-all-start = ((s32[8,1,5]{2,1,0:T(1,128)}), s32[8,1,5]{2,1,0:T(1,128)S(1)}, u32[]{:S(2)}, u32[]{:S(2)}) async-start(s32[8,1,5]{2,1,0:T(1,128)} %bitcast), calls=%async_computation | async-start | bytes 8192 | tf_op jit(solution)/shard_map/all_to_all | solution.py:764
  9.1 3.4 %copy-start.1 = (bf16[1024,192]{0,1:T(8,128)(2,1)S(1)}, bf16[1024,192]{0,1:T(8,128)(2,1)}, u32[]{:S(2)}) copy-start(bf16[1024,192]{0,1:T(8,128)(2,1)} %param.13) | copy-start | bytes 1179652
  286.3 8.7 %copy-start.4 = (f32[8,128]{1,0:T(8,128)S(1)}, f32[8,128]{1,0:T(8,128)}, u32[]{:S(2)}) copy-start(f32[8,128]{1,0:T(8,128)} %get-tuple-element.16) | copy-start | bytes 12292
  286.3 9.3 %copy-start.3 = (f32[8,128]{1,0:T(8,128)S(1)}, f32[8,128]{1,0:T(8,128)}, u32[]{:S(2)}) copy-start(f32[8,128]{1,0:T(8,128)} %get-tuple-element.17) | copy-start | bytes 12292

commit v2 on v1

--- a/solution.py
+++ b/solution.py
@@ -96,6 +96,9 @@
             self.landed(p).wait_recv()
             self.passed(p).start()
 
+    def forward_far(self):
+        pass
+
     def finish(self):
         j = self.half - 1
         at = self.slot(self.partner)
@@ -111,6 +114,65 @@
             self.passed(p).wait_send()
 
 
+def flip(index, size):
+    return index + size - 2 * size * lax.rem(index // size, 2)
+
+
+class Relay:
+    def __init__(self, src, slot, rows, send, recv):
+        me = lax.axis_index("narrow")
+        self.me, self.sib, self.xn, self.yn = me, flip(me, 1), flip(me, 2), flip(me, 4)
+        self.far = flip(self.xn, 4)
+        self.src, self.slot, self.send, self.recv = src, slot, send, recv
+        self.low, self.high, self.full = pl.ds(0, rows // 2), pl.ds(rows // 2, rows // 2), pl.ds(0, rows)
+        self.rows = rows
+
+    def copy(self, j, src, dst, target):
+        return remote(src, dst, self.send(j), self.recv(j), to_narrow(target))
+
+    def through(self, j, owner, part, target):
+        at = self.slot(owner, part)
+        return self.copy(j, at, at, target)
+
+    def own(self):
+        at = self.slot(self.me, 0)
+        return [self.copy(j, self.src, at, t) for j, t in enumerate((self.xn, self.yn, self.sib))]
+
+    def relays(self):
+        return [
+            self.through(3, self.xn, 1, self.yn),
+            self.through(4, self.yn, 2, self.xn),
+            self.through(5, self.xn, 0, self.sib),
+            self.through(6, self.yn, 0, self.sib),
+        ]
+
+    def corner(self):
+        return self.through(7, self.far, 0, self.sib)
+
+    def start(self):
+        for c in self.own():
+            c.start()
+
+    def forward(self):
+        self.through(0, self.xn, 0, self.xn).wait_recv()
+        self.through(1, self.yn, 0, self.yn).wait_recv()
+        for c in self.relays():
+            c.start()
+
+    def forward_far(self):
+        self.through(3, self.far, 1, self.yn).wait_recv()
+        self.through(4, self.far, 2, self.xn).wait_recv()
+        self.corner().start()
+
+    def finish(self):
+        self.through(2, self.sib, 0, self.sib).wait_recv()
+        self.through(5, flip(self.sib, 2), 0, self.sib).wait_recv()
+        self.through(6, flip(self.sib, 4), 0, self.sib).wait_recv()
+        self.through(7, flip(self.far, 1), 0, self.sib).wait_recv()
+        for c in self.own() + self.relays() + [self.corner()]:
+            c.wait_send()
+
+
 def diagonal():
     return lax.broadcasted_iota(jnp.int32, (BLK, BLK), 0) == lax.broadcasted_iota(
         jnp.int32, (BLK, BLK), 1
@@ -130,7 +192,9 @@
     nu_ref,
     x_ref,
     y_ref,
+    ask_ref,
     pot_ref,
+    got_ref,
     xall_ref,
     yall_ref,
     frag,
@@ -157,6 +221,8 @@
     kr,
     ls,
     lr,
+    qs,
+    qr,
     loc,
 ):
     me_n = lax.axis_index("narrow")
@@ -185,24 +251,32 @@
         c = remote(ct_ref, panel.at[me_w], ps.at[p - 1], pr.at[p - 1], to_wide(lax.rem(me_w + p, w)))
         c.start()
         panels.append(c)
+    asks = []
+    for p in range(1, n):
+        to = lax.rem(me_n + p, n)
+        c = remote(ask_ref.at[to], got_ref.at[me_n], qs.at[p - 1], qr.at[p - 1], to_narrow(to))
+        c.start()
+        asks.append(c)
+    local.append(pltpu.make_async_copy(ask_ref.at[me_n], got_ref.at[me_n], loc.at[4]))
     for c in local:
         c.start()
 
     def bulk(which, c):
         src, dst = ((y_ref, yall_ref), (x_ref, xall_ref))[which]
-        at = pl.ds(pl.multiple_of(c * step_rows, step_rows), step_rows)
-        return Gather(
-            n,
-            src.at[at],
-            lambda i: dst.at[i, at],
-            lambda j: bs.at[which, c, j],
-            lambda j: br.at[which, c, j],
-        )
-
-    fg.forward()
+        first = pl.multiple_of(c * step_rows, step_rows)
+        at = pl.ds(first, step_rows)
+        send, recv = (lambda j: bs.at[which, c, j]), (lambda j: br.at[which, c, j])
+        if n != 8:
+            return Gather(n, src.at[at], lambda i: dst.at[i, at], send, recv)
+        low = pl.ds(first, step_rows // 2)
+        high = pl.ds(pl.multiple_of(first + step_rows // 2, step_rows // 2), step_rows // 2)
+        parts = (at, low, high)
+        return Relay(src.at[at], lambda i, part: dst.at[i, parts[part]], step_rows, send, recv)
+
     for c in range(2):
         bulk(0, c).start()
         bulk(1, c).start()
+    fg.forward()
     fg.finish()
     for p in range(1, w):
         at = panel.at[lax.rem(me_w + w - p, w)]
@@ -234,7 +308,7 @@
             sq = sq + jnp.sum(v * v, axis=1, keepdims=True)
         bsq[:, g * BLK : (g + 1) * BLK] = as_row(sq, diag) * (UNIT / features)
     gcol[...] = -bsq[...]
-    sub = 32
+    sub = 16
     cg = cols // BLK
 
     def turn(it, carry):
@@ -249,8 +323,8 @@
                 z = jnp.sum(jnp.exp2(t - m), axis=1, keepdims=True)
                 ms.append(m)
                 zs.append(z)
-            row_out[it, pl.ds(g, 1), :] = as_row(jnp.concatenate(ms, axis=0), diag)
-            row_out[it, pl.ds(groups + g, 1), :] = as_row(jnp.concatenate(zs, axis=0), diag)
+            whole = jnp.concatenate(ms, axis=0) + jnp.log2(jnp.concatenate(zs, axis=0))
+            row_out[it, pl.ds(g, 1), :] = as_row(whole, diag)
             return c2
 
         lax.fori_loop(0, groups, row_group, 0)
@@ -268,16 +342,19 @@
         bulk(0, it + 2).start()
         for c in sent:
             c.wait_recv()
-        top = row_out[it, 0:groups, :]
+        top = row_out[it]
         for p in range(n - 1):
-            top = jnp.maximum(top, row_in[it, p, 0:groups, :])
-        total = row_out[it, groups : 2 * groups, :] * jnp.exp2(row_out[it, 0:groups, :] - top)
+            top = jnp.maximum(top, row_in[it, p])
+        total = jnp.exp2(row_out[it] - top)
         for p in range(n - 1):
-            total = total + row_in[it, p, groups : 2 * groups, :] * jnp.exp2(
-                row_in[it, p, 0:groups, :] - top
-            )
+            total = total + jnp.exp2(row_in[it, p] - top)
         frow[...] = jnp.log2(mu_ref[...]) - (top + jnp.log2(total))
         bulk(0, it).forward()
+
+        @pl.when(it >= 1)
+        def _():
+            bulk(0, it - 1).forward_far()
+
 
         def spread(g, c2):
             line = jnp.broadcast_to(frow[pl.ds(g, 1), :], (BLK, BLK))
@@ -287,35 +364,24 @@
         lax.fori_loop(0, groups, spread, 0)
         span = 64
 
-        def top_step(r, tops):
+        def column_step(r, kept):
             start = pl.multiple_of(r * span, span)
             f = frep[pl.ds(start, span), :]
             out = []
             for c in range(cg):
-                t = f + tile[pl.ds(start, span), c * BLK : (c + 1) * BLK]
-                out.append(jnp.maximum(tops[c], jnp.max(t.reshape(span // 8, 8, BLK), axis=0)))
+                old, acc = kept[2 * c], kept[2 * c + 1]
+                t = (f + tile[pl.ds(start, span), c * BLK : (c + 1) * BLK]).reshape(span // 8, 8, BLK)
+                new = jnp.maximum(old, jnp.max(t, axis=0))
+                acc = acc * jnp.exp2(old - new) + jnp.sum(jnp.exp2(t - new[None]), axis=0)
+                out += [new, acc]
             return tuple(out)
 
-        tops = lax.fori_loop(
-            0, rows // span, top_step, tuple(jnp.full((8, BLK), NEG, jnp.float32) for _ in range(cg))
-        )
-        tops = tuple(jnp.broadcast_to(jnp.max(t, axis=0, keepdims=True), (8, BLK)) for t in tops)
-
-        def sum_step(r, sums):
-            start = pl.multiple_of(r * span, span)
-            f = frep[pl.ds(start, span), :]
-            out = []
-            for c in range(cg):
-                t = (f + tile[pl.ds(start, span), c * BLK : (c + 1) * BLK]).reshape(span // 8, 8, BLK)
-                out.append(sums[c] + jnp.sum(jnp.exp2(t - tops[c][None]), axis=0))
-            return tuple(out)
-
-        sums = lax.fori_loop(
-            0, rows // span, sum_step, tuple(jnp.zeros((8, BLK), jnp.float32) for _ in range(cg))
-        )
+        begin = (jnp.full((8, BLK), NEG, jnp.float32), jnp.zeros((8, BLK), jnp.float32))
+        kept = lax.fori_loop(0, rows // span, column_step, begin * cg)
         for c in range(cg):
-            col_out[it, 0:1, c * BLK : (c + 1) * BLK] = tops[c][0:1]
-            col_out[it, 1:2, c * BLK : (c + 1) * BLK] = jnp.sum(sums[c], axis=0, keepdims=True)
+            top = jnp.max(kept[2 * c], axis=0, keepdims=True)
+            acc = jnp.sum(kept[2 * c + 1] * jnp.exp2(kept[2 * c] - top), axis=0, keepdims=True)
+            col_out[it, :, c * BLK : (c + 1) * BLK] = top + jnp.log2(acc)
         csent = []
         for p in range(1, w):
             c = remote(
@@ -330,14 +396,19 @@
         bulk(1, it + 2).start()
         for c in csent:
             c.wait_recv()
-        top = col_out[it, 0:1, :]
+        top = col_out[it]
         for p in range(w - 1):
-            top = jnp.maximum(top, col_in[it, p, 0:1, :])
-        total = col_out[it, 1:2, :] * jnp.exp2(col_out[it, 0:1, :] - top)
+            top = jnp.maximum(top, col_in[it, p])
+        total = jnp.exp2(col_out[it] - top)
         for p in range(w - 1):
-            total = total + col_in[it, p, 1:2, :] * jnp.exp2(col_in[it, p, 0:1, :] - top)
+            total = total + jnp.exp2(col_in[it, p] - top)
         gcol[...] = jnp.log2(nu_ref[...]) - (top + jnp.log2(total))
         bulk(1, it).forward()
+
+        @pl.when(it >= 1)
+        def _():
+            bulk(1, it - 1).forward_far()
+
         for c in sent:
             c.wait_send()
         for c in csent:
@@ -363,6 +434,9 @@
     for c in range(ITC, chunks):
         bulk(0, c).forward()
         bulk(1, c).forward()
+    for c in range(ITC - 1, chunks):
+        bulk(0, c).forward_far()
+        bulk(1, c).forward_far()
 
     def close(c, carry):
         bulk(0, c).finish()
@@ -370,11 +444,16 @@
         return carry
 
     lax.fori_loop(0, chunks, close, 0)
-    local[2].wait()
-    local[3].wait()
-
-
-def coarse_call(n, w, cs, ct, mu, nu, x, y):
+    for c in local[2:]:
+        c.wait()
+    for p in range(1, n):
+        at = got_ref.at[lax.rem(me_n + n - p, n)]
+        remote(at, at, qs.at[p - 1], qr.at[p - 1], to_narrow(lax.rem(me_n + p, n))).wait_recv()
+    for c in asks:
+        c.wait_send()
+
+
+def coarse_call(n, w, cs, ct, mu, nu, x, y, asks):
     rb = cs.shape[1]
     cols, part = ct.shape
     rows = rb * n
@@ -388,11 +467,12 @@
         functools.partial(coarse_kernel, n, w),
         out_shape=(
             jax.ShapeDtypeStruct((n, 1, cols), f32),
+            jax.ShapeDtypeStruct(asks.shape, asks.dtype),
             jax.ShapeDtypeStruct((n,) + x.shape, x.dtype),
             jax.ShapeDtypeStruct((n,) + y.shape, y.dtype),
         ),
-        in_specs=[vm] * 6,
-        out_specs=(vm, anyspace, anyspace),
+        in_specs=[vm] * 7,
+        out_specs=(vm, vm, anyspace, anyspace),
         scratch_shapes=[
             pltpu.VMEM((n, w, rb, part), cs.dtype),
             pltpu.VMEM((w, cols, part), ct.dtype),
@@ -401,30 +481,32 @@
             pltpu.VMEM((groups, BLK), f32),
             pltpu.VMEM((1, cols), f32),
             pltpu.VMEM((1, cols), f32),
-            pltpu.VMEM((ITC, 2 * groups, BLK), f32),
-            pltpu.VMEM((ITC, n - 1, 2 * groups, BLK), f32),
-            pltpu.VMEM((ITC, 2, cols), f32),
-            pltpu.VMEM((ITC, w - 1, 2, cols), f32),
+            pltpu.VMEM((ITC, groups, BLK), f32),
+            pltpu.VMEM((ITC, n - 1, groups, BLK), f32),
+            pltpu.VMEM((ITC, 1, cols), f32),
+            pltpu.VMEM((ITC, w - 1, 1, cols), f32),
             pltpu.VMEM((n - 1, 1, cols), f32),
             dma((n - 1,)),
             dma((n - 1,)),
             dma((w - 1,)),
             dma((w - 1,)),
-            dma((2, chunks, n - 1)),
-            dma((2, chunks, n - 1)),
+            dma((2, chunks, max(n - 1, 8))),
+            dma((2, chunks, max(n - 1, 8))),
             dma((ITC, n - 1)),
             dma((ITC, n - 1)),
             dma((ITC, w - 1)),
             dma((ITC, w - 1)),
             dma((n - 1,)),
             dma((n - 1,)),
-            dma((4,)),
+            dma((n - 1,)),
+            dma((n - 1,)),
+            dma((5,)),
         ],
         compiler_params=pltpu.CompilerParams(
             collective_id=0, has_side_effects=True, vmem_limit_bytes=VMEM_LIMIT
         ),
         name="coarse",
-    )(cs, ct, mu, nu, x, y)
+    )(cs, ct, mu, nu, x, y, asks)
 
 
 def score_kernel(unit, row_pick, index_ref, own_ref, *refs):
@@ -545,13 +627,13 @@
             pots[fx][pl.ds(me_n * sb + b, 1), :] = as_row(-(top + jnp.log2(total)), diag)
             return c2
 
-        lax.fori_loop(0, sb, src_block, 0)
+        lax.fori_loop(0, sb, src_block, 0, unroll=2)
         share(fx, sb)
         arrive(fx, sb)
 
         def slot_step(s, c2, fx=fx):
-            for u in range(2):
-                e = s * 2 + u
+            for u in range(GROUP):
+                e = s * GROUP + u
                 t = mt_ref[e] + pots[fx][pl.ds(tmeta[0, e], 1), :]
                 top = jnp.max(t, axis=1, keepdims=True)
                 total = jnp.sum(jnp.exp2(t - top), axis=1, keepdims=True)
@@ -559,7 +641,7 @@
                 zbuf[pl.ds(e, 1), :] = as_row(total, diag)
             return c2
 
-        lax.fori_loop(0, slots // 2, slot_step, 0)
+        lax.fori_loop(0, slots // GROUP, slot_step, 0)
         live = live_ref[...]
         m_all = mbuf[...]
         z_all = zbuf[...]
@@ -761,8 +843,12 @@
     code = local_block + tb * (index // LIST) + 1
     hit = slot_of[None, :] == jnp.arange(slots, dtype=jnp.int32)[:, None]
     requests = jnp.sum(jnp.where(hit, code[None, :], 0), axis=1).reshape(n, capacity)
-    asked = lax.all_to_all(requests, "narrow", split_axis=0, concat_axis=0, tiled=True)
-    asked = asked.reshape(-1) - 1
+    cs = centroids_src.reshape(centroids_src.shape[0], w, -1).transpose(1, 0, 2)
+    mu = sender_mean_measure.reshape(-1, BLK)
+    nu = recipient_mean_measure.reshape(1, -1)
+    asks = jnp.pad(requests, ((0, 0), (0, BLK - capacity))).reshape(n, 1, BLK)
+    coarse, got, xall, yall = coarse_call(n, w, cs, centroids_tgt, mu, nu, sources, targets, asks)
+    asked = got[:, 0, :capacity].reshape(-1) - 1
     alive = asked >= 0
     clipped = jnp.maximum(asked, 0)
     from_block = (jnp.arange(slots, dtype=jnp.int32) // capacity) * sb + clipped // tb
@@ -771,10 +857,6 @@
     live = jnp.broadcast_to(jnp.where(alive, to_block, -1)[:, None], (slots, BLK))
     smeta = owner_of * tb + local_block
 
-    cs = centroids_src.reshape(centroids_src.shape[0], w, -1).transpose(1, 0, 2)
-    mu = sender_mean_measure.reshape(-1, BLK)
-    nu = recipient_mean_measure.reshape(1, -1)
-    coarse, xall, yall = coarse_call(n, w, cs, centroids_tgt, mu, nu, sources, targets)
     xall = xall.reshape(n * sb, BLK, feature_count)
     yall = yall.reshape(n * tb, BLK, feature_count)
     src_blocks = sources.reshape(sb, BLK, feature_count)

time: 297 us -> 277 us (0.933)
  Pallas kernels: 278 us -> 262 us
  starting transfers between devices: 5.2 us -> 0 us
    pallas_call x1, Pallas kernels: 50.3 us -> 41.1 us  [fine_call(): pl.pallas_call(functools.partial(fine_kernel, n, w), out_shape=(jax.Shape...]
    pallas_call x1, Pallas kernels: 187 us -> 180 us  [coarse_call(): pl.pallas_call(functools.partial(coarse_kernel, n, w), out_shape=(jax.Sha...]
    all_to_all x1 -> x0, starting transfers between devices: 5.2 us -> none  [body(): lax.all_to_all(requests, 'narrow', split_axis=0, concat_axis=0, tiled=True)]
  transfers between devices with their start and end apart: 1 -> 0, of which waited for: 0 -> 0; matrix products, arithmetic and copies ran while one was open for 2% -> 0% of each run, Pallas kernels for 66% -> 0%
where the time goes in v2:
time: 277 us; the launch traced here: 276 us
  Pallas kernels  262 us (95%)
  local copies, waits for them, and re-layouts  7.7 us (3%)
  other arithmetic  6.29 us (2%)
    pallas_call x1, Pallas kernels, coarse_call(): pl.pallas_call(functools.partial(coarse_kernel, n, w), out_shape=(jax.Sha...  180 us
    pallas_call x1, Pallas kernels, fine_call(): pl.pallas_call(functools.partial(fine_kernel, n, w), out_shape=(jax.Shape...  41.1 us
    pallas_call x2, Pallas kernels, score_call(): pl.pallas_call(functools.partial(score_kernel, unit, row_pick), out_shape...  20 us
    pallas_call x1, Pallas kernels, target_mean(): pl.pallas_call(functools.partial(target_mean_kernel, tb), out_shape=jax.S...  11.4 us
    pallas_call x1, Pallas kernels, source_mean(): pl.pallas_call(source_mean_kernel, out_shape=jax.ShapeDtypeStruct((entrie...  8.7 us

profile of v2, /device:TPU:0, one launch (start us, length us, event | category | flops | bytes accessed | tf_op | source)
XLA Modules:
  0.0 276.3 jit_solution(2527689741794023033)
XLA Ops:
  0.6 0.0 copy-start
  0.6 0.0 copy-start.2
  0.7 0.9 copy.21
  1.5 0.1 reshape.405
  1.6 0.1 reshape.404
  1.7 0.6 fusion.1.index_ref.meta
  2.3 0.5 multiply_add_fusion.1
  2.9 0.2 convert_reduce_fusion
  3.1 0.1 select_reduce_fusion
  3.2 0.1 reshape.409
  3.2 0.6 pad.4
  3.9 0.0 copy-start.1
  3.9 1.8 multiply_reduce_fusion.1
  5.7 0.0 copy-done
  5.7 0.4 multiply_reduce_fusion
  6.1 0.6 multiply_bitcast_fusion
  6.7 0.0 copy-done.2
  6.7 0.2 copy.23
  6.9 1.0 copy.24
  7.9 0.0 copy-done.1
  7.9 1.0 copy.25.ct_ref
  8.9 180.4 %coarse.1 = (f32[8,1,1024]{2,1,0:T(1,128)}, s32[8,1,128]{2,1,0:T(1,128)}, bf16[8,1024,768]{2,1,0:T(8,128)(2,1)}, bf16[8,1024,768]{2,1,0:T(8,128)(2,1)}) custom-call(bf16[4,256,192]{2,1,0:T(8,128)(2,1)} %bitcast.37, bf16[1024,192]{1,0:T(8,128)(2,1)} %copy.25.ct_ref, f32[16,128]{1,0:T(8,128)} %bitcast.43, f32[1,1024]{1,0:T(1,128)} %bitcast.46, ...), custom_call_target="tpu_custom_call" | custom-call | tf_op jit(solution)/shard_map/coarse/pallas_call | solution.py:466
  189.2 0.7 compare_reduce_fusion
  190.0 0.1 ge.11
  190.0 0.1 ne.239
  190.1 0.7 shift-right-logical_reduce_fusion
  190.8 0.1 div.60
  190.9 0.1 rem.142
  191.0 0.6 pad_add_fusion.index_ref.tmeta.meta
  191.6 0.1 rem.143
  191.7 0.7 broadcast_in_dim.18.live_ref
  192.4 1.5 copy.26
  193.9 9.2 %scores.2.ms_ref = f32[32,128,128]{2,1,0:T(8,128)} custom-call(s32[1,32]{1,0:T(1,128)} %fusion.1.index_ref.meta, bf16[8,128,768]{2,1,0:T(8,128)(2,1)} %bitcast.35, bf16[64,128,768]{2,1,0:T(8,128)(2,1)} %bitcast.19, bf16[64,128,768]{2,1,0:T(8,128)(2,1)} %bitcast.20, bf16[64,128,768]{2,1,0:T(8,128)(2,1)} %bitcast.21, bf16[64,128,768]{2,1,0:T(8,128)(2,1)} %bitcast.22), custom_call_target="tpu_custom_call" | custom-call | tf_op jit(solution)/shard_map/scores/pallas_call | solution.py:526
  203.0 10.8 %scores.3.mt_ref = f32[40,128,128]{2,1,0:T(8,128)} custom-call(s32[2,40]{1,0:T(2,128)} %pad_add_fusion.index_ref.tmeta.meta, bf16[8,128,768]{2,1,0:T(8,128)(2,1)} %bitcast.36, bf16[64,128,768]{2,1,0:T(8,128)(2,1)} %bitcast.27, bf16[64,128,768]{2,1,0:T(8,128)(2,1)} %bitcast.28, bf16[64,128,768]{2,1,0:T(8,128)(2,1)} %bitcast.29, bf16[64,128,768]{2,1,0:T(8,128)(2,1)} %bitcast.30), custom_call_target="tpu_custom_call" | custom-call | tf_op jit(solution)/shard_map/scores/pallas_call | solution.py:526
  213.9 41.1 %fine.1 = (f32[8,128]{1,0:T(8,128)}, f32[8,128]{1,0:T(8,128)}, bf16[32,128,128]{2,1,0:T(8,128)(2,1)}, bf16[40,128,128]{2,1,0:T(8,128)(2,1)}) custom-call(s32[32]{0:T(128)} %get-tuple-element.26.smeta, s32[2,40]{1,0:T(2,128)} %pad_add_fusion.index_ref.tmeta.meta, f32[32,128,128]{2,1,0:T(8,128)} %scores.2.ms_ref, f32[40,128,128]{2,1,0:T(8,128)} %scores.3.mt_ref, ...), custom_call_target="tpu_custom_call" | custom-call | tf_op jit(solution)/shard_map/fine/pallas_call | solution.py:693
  255.0 11.4 %target_mean.1 = bf16[1024,768]{1,0:T(8,128)(2,1)} custom-call(s32[2,40]{1,0:T(2,128)} %pad_add_fusion.index_ref.tmeta.meta, bf16[40,128,128]{2,1,0:T(8,128)(2,1)} %get-tuple-element.17.plan_ref, bf16[64,128,768]{2,1,0:T(8,128)(2,1)} %bitcast.31, bf16[64,128,768]{2,1,0:T(8,128)(2,1)} %bitcast.32, bf16[64,128,768]{2,1,0:T(8,128)(2,1)} %bitcast.33, ...), custom_call_target="tpu_custom_call" | custom-call | tf_op jit(solution)/shard_map/target_mean/pallas_call | solution.py:785
  266.4 0.0 copy-start.4
  266.4 0.0 copy-start.3
  266.4 8.7 %source_mean.1 = bf16[1024,768]{1,0:T(8,128)(2,1)} custom-call(s32[1,32]{1,0:T(1,128)} %fusion.1.index_ref.meta, bf16[32,128,128]{2,1,0:T(8,128)(2,1)} %get-tuple-element.16.plan_ref, bf16[64,128,768]{2,1,0:T(8,128)(2,1)} %bitcast.23, bf16[64,128,768]{2,1,0:T(8,128)(2,1)} %bitcast.24, bf16[64,128,768]{2,1,0:T(8,128)(2,1)} %bitcast.25, ...), custom_call_target="tpu_custom_call" | custom-call | tf_op jit(solution)/shard_map/source_mean/pallas_call | solution.py:738
  275.1 0.0 copy-done.4
  275.1 0.6 copy.29
  275.7 0.0 copy-done.3
  275.7 0.6 copy.30
  (4 shorter events, 0.0 us)
Async XLA Ops:
  0.6 5.1 %copy-start = (bf16[1024,768]{1,0:T(8,128)(2,1)S(1)}, bf16[1024,768]{1,0:T(8,128)(2,1)}, u32[]{:S(2)}) copy-start(bf16[1024,768]{1,0:T(8,128)(2,1)} %y_ref.1) | copy-start | bytes 4718596
  0.6 6.0 %copy-start.2 = (bf16[256,768]{1,0:T(8,128)(2,1)S(1)}, bf16[256,768]{1,0:T(8,128)(2,1)}, u32[]{:S(2)}) copy-start(bf16[256,768]{1,0:T(8,128)(2,1)} %param.12) | copy-start | bytes 1179652
  3.9 4.0 %copy-start.1 = (bf16[1024,192]{0,1:T(8,128)(2,1)S(1)}, bf16[1024,192]{0,1:T(8,128)(2,1)}, u32[]{:S(2)}) copy-start(bf16[1024,192]{0,1:T(8,128)(2,1)} %param.13) | copy-start | bytes 1179652
  266.4 8.7 %copy-start.4 = (f32[8,128]{1,0:T(8,128)S(1)}, f32[8,128]{1,0:T(8,128)}, u32[]{:S(2)}) copy-start(f32[8,128]{1,0:T(8,128)} %get-tuple-element.18) | copy-start | bytes 12292
  266.4 9.3 %copy-start.3 = (f32[8,128]{1,0:T(8,128)S(1)}, f32[8,128]{1,0:T(8,128)}, u32[]{:S(2)}) copy-start(f32[8,128]{1,0:T(8,128)} %get-tuple-element.19) | copy-start | bytes 12292

commit v3 on v2

--- a/solution.py
+++ b/solution.py
@@ -15,7 +15,7 @@
 HEAT = 0.02
 LOG2E = math.log2(math.e)
 UNIT = LOG2E / HEAT
-GROUP = 4
+GROUP = 8
 VMEM_LIMIT = 60 * 1024 * 1024
 NEG = -jnp.inf
 NT = (((1,), (1,)), ((), ()))
@@ -273,23 +273,22 @@
         parts = (at, low, high)
         return Relay(src.at[at], lambda i, part: dst.at[i, parts[part]], step_rows, send, recv)
 
-    for c in range(2):
+    ahead = chunks // 2
+    for c in range(ahead):
         bulk(0, c).start()
         bulk(1, c).start()
     fg.forward()
-    fg.finish()
     for p in range(1, w):
         at = panel.at[lax.rem(me_w + w - p, w)]
         remote(at, at, ps.at[p - 1], pr.at[p - 1], to_wide(lax.rem(me_w + p, w))).wait_recv()
-    for c in panels:
-        c.wait_send()
     local[0].wait()
     local[1].wait()
 
     unit = 2.0 * UNIT / features
     half = min(cols, 512)
 
-    def product(i, carry):
+    def product(j, carry, first):
+        i = lax.rem(first + 2 * j, n)
         for c in range(cols // half):
             acc = None
             for k in range(w):
@@ -300,7 +299,17 @@
             tile[pl.ds(pl.multiple_of(i * rb, rb), rb), c * half : (c + 1) * half] = acc * unit
         return carry
 
-    lax.fori_loop(0, n, product, 0)
+    lax.fori_loop(0, n // 2, functools.partial(product, first=me_n), 0)
+    bulk(0, 0).forward()
+    bulk(1, 0).forward()
+    fg.finish()
+    lax.fori_loop(0, n // 2, functools.partial(product, first=fg.partner), 0)
+    for c in panels:
+        c.wait_send()
+    bulk(0, 1).forward()
+    bulk(1, 1).forward()
+    bulk(0, 0).forward_far()
+    bulk(1, 0).forward_far()
     for g in range(cols // BLK):
         sq = jnp.zeros((BLK, 1), jnp.float32)
         for k in range(w):
@@ -327,7 +336,7 @@
             row_out[it, pl.ds(g, 1), :] = as_row(whole, diag)
             return c2
 
-        lax.fori_loop(0, groups, row_group, 0)
+        lax.fori_loop(0, groups, row_group, 0, unroll=4)
         sent = []
         for p in range(1, n):
             c = remote(
@@ -339,7 +348,11 @@
             )
             c.start()
             sent.append(c)
-        bulk(0, it + 2).start()
+
+        @pl.when(it + ahead < chunks)
+        def _():
+            bulk(0, it + ahead).start()
+
         for c in sent:
             c.wait_recv()
         top = row_out[it]
@@ -349,11 +362,8 @@
         for p in range(n - 1):
             total = total + jnp.exp2(row_in[it, p] - top)
         frow[...] = jnp.log2(mu_ref[...]) - (top + jnp.log2(total))
-        bulk(0, it).forward()
-
-        @pl.when(it >= 1)
-        def _():
-            bulk(0, it - 1).forward_far()
+        bulk(0, it + 2).forward()
+        bulk(0, it + 1).forward_far()
 
 
         def spread(g, c2):
@@ -361,7 +371,7 @@
             frep[pl.ds(pl.multiple_of(g * BLK, BLK), BLK), :] = line.T
             return c2
 
-        lax.fori_loop(0, groups, spread, 0)
+        lax.fori_loop(0, groups, spread, 0, unroll=4)
         span = 64
 
         def column_step(r, kept):
@@ -393,7 +403,11 @@
             )
             c.start()
             csent.append(c)
-        bulk(1, it + 2).start()
+
+        @pl.when(it + ahead < chunks)
+        def _():
+            bulk(1, it + ahead).start()
+
         for c in csent:
             c.wait_recv()
         top = col_out[it]
@@ -403,11 +417,8 @@
         for p in range(w - 1):
             total = total + jnp.exp2(col_in[it, p] - top)
         gcol[...] = jnp.log2(nu_ref[...]) - (top + jnp.log2(total))
-        bulk(1, it).forward()
-
-        @pl.when(it >= 1)
-        def _():
-            bulk(1, it - 1).forward_far()
+        bulk(1, it + 2).forward()
+        bulk(1, it + 1).forward_far()
 
         for c in sent:
             c.wait_send()
@@ -431,12 +442,8 @@
         pot_ref[lax.rem(me_n + n - p, n)] = last_in[p - 1]
     for c in last:
         c.wait_send()
-    for c in range(ITC, chunks):
-        bulk(0, c).forward()
-        bulk(1, c).forward()
-    for c in range(ITC - 1, chunks):
-        bulk(0, c).forward_far()
-        bulk(1, c).forward_far()
+    bulk(0, chunks - 1).forward_far()
+    bulk(1, chunks - 1).forward_far()
 
     def close(c, carry):
         bulk(0, c).finish()
@@ -627,7 +634,7 @@
             pots[fx][pl.ds(me_n * sb + b, 1), :] = as_row(-(top + jnp.log2(total)), diag)
             return c2
 
-        lax.fori_loop(0, sb, src_block, 0, unroll=2)
+        lax.fori_loop(0, sb, src_block, 0, unroll=4)
         share(fx, sb)
         arrive(fx, sb)
 
@@ -665,7 +672,7 @@
         pt_ref[s] = jnp.where(alive, jnp.exp2(t), 0.0).astype(jnp.bfloat16)
         return c2
 
-    lax.fori_loop(0, slots, target_plan, 0)
+    lax.fori_loop(0, slots, target_plan, 0, unroll=4)
     fpot_ref[...] = (pots[fx][region(me_n, sb), :] + asq_ref[...]) * (1.0 / UNIT)
     gpot_ref[...] = (own_g[...] + bsq_ref[...]) * (1.0 / UNIT)
     arrive(gx, tb)
@@ -679,7 +686,7 @@
             ps_ref[e] = jnp.exp2(t).astype(jnp.bfloat16)
         return c2
 
-    lax.fori_loop(0, sb, source_plan, 0)
+    lax.fori_loop(0, sb, source_plan, 0, unroll=2)
 
 
 def fine_call(n, w, smeta, tmeta, ms, mt, live, coarse, clusters, asq, bsq):
@@ -806,7 +813,7 @@
 
 
 def own_block_of_entry(meta_ref, step, l):
-    return step
+    return (step * GROUP + l) // LIST
 
 
 def own_block_of_slot(meta_ref, step, l):

time: 277 us -> 249 us (0.90)
  Pallas kernels: 262 us -> 234 us
    pallas_call x1, Pallas kernels: 180 us -> 159 us  [coarse_call(): pl.pallas_call(functools.partial(coarse_kernel, n, w), out_shape=(jax.Sha...]
    pallas_call x2, Pallas kernels: 20 us -> 16.3 us  [score_call(): pl.pallas_call(functools.partial(score_kernel, unit, row_pick), out_shape...]
where the time goes in v3:
time: 249 us; the launch traced here: 248 us
  Pallas kernels  234 us (94%)
  local copies, waits for them, and re-layouts  7.7 us (3%)
  other arithmetic  6.29 us (3%)
    pallas_call x1, Pallas kernels, coarse_call(): pl.pallas_call(functools.partial(coarse_kernel, n, w), out_shape=(jax.Sha...  159 us
    pallas_call x1, Pallas kernels, fine_call(): pl.pallas_call(functools.partial(fine_kernel, n, w), out_shape=(jax.Shape...  39.9 us
    pallas_call x2, Pallas kernels, score_call(): pl.pallas_call(functools.partial(score_kernel, unit, row_pick), out_shape...  16.3 us
    pallas_call x1, Pallas kernels, target_mean(): pl.pallas_call(functools.partial(target_mean_kernel, tb), out_shape=jax.S...  9.91 us
    pallas_call x1, Pallas kernels, source_mean(): pl.pallas_call(source_mean_kernel, out_shape=jax.ShapeDtypeStruct((entrie...  8.58 us

profile of v3, /device:TPU:0, one launch (start us, length us, event | category | flops | bytes accessed | tf_op | source)
XLA Modules:
  0.0 248.5 jit_solution(14489311162204883642)
XLA Ops:
  0.6 0.0 copy-start
  0.6 0.0 copy-start.2
  0.7 0.9 copy.21
  1.5 0.1 reshape.405
  1.6 0.1 reshape.404
  1.7 0.6 fusion.1.index_ref.meta
  2.3 0.5 multiply_add_fusion.1
  2.9 0.2 convert_reduce_fusion
  3.1 0.1 select_reduce_fusion
  3.2 0.1 reshape.409
  3.2 0.6 pad.4
  3.9 0.0 copy-start.1
  3.9 1.8 multiply_reduce_fusion.1
  5.7 0.0 copy-done
  5.7 0.4 multiply_reduce_fusion
  6.1 0.6 multiply_bitcast_fusion
  6.7 0.0 copy-done.2
  6.7 0.2 copy.23
  6.9 1.0 copy.24
  7.9 0.0 copy-done.1
  7.9 1.0 copy.25.ct_ref
  8.9 159.0 %coarse.1 = (f32[8,1,1024]{2,1,0:T(1,128)}, s32[8,1,128]{2,1,0:T(1,128)}, bf16[8,1024,768]{2,1,0:T(8,128)(2,1)}, bf16[8,1024,768]{2,1,0:T(8,128)(2,1)}) custom-call(bf16[4,256,192]{2,1,0:T(8,128)(2,1)} %bitcast.49, bf16[1024,192]{1,0:T(8,128)(2,1)} %copy.25.ct_ref, f32[16,128]{1,0:T(8,128)} %bitcast.55, f32[1,1024]{1,0:T(1,128)} %bitcast.58, ...), custom_call_target="tpu_custom_call" | custom-call | tf_op jit(solution)/shard_map/coarse/pallas_call | solution.py:473
  167.9 0.7 compare_reduce_fusion
  168.6 0.1 ge.11
  168.7 0.1 ne.239
  168.8 0.7 shift-right-logical_reduce_fusion
  169.5 0.1 div.60
  169.6 0.1 rem.142
  169.7 0.6 pad_add_fusion.index_ref.tmeta.meta
  170.3 0.1 rem.143
  170.4 0.7 broadcast_in_dim.18.live_ref
  171.1 1.5 copy.26
  172.5 7.4 %scores.2.ms_ref = f32[32,128,128]{2,1,0:T(8,128)} custom-call(s32[1,32]{1,0:T(1,128)} %fusion.1.index_ref.meta, bf16[8,128,768]{2,1,0:T(8,128)(2,1)} %bitcast.47, bf16[64,128,768]{2,1,0:T(8,128)(2,1)} %bitcast.35, bf16[64,128,768]{2,1,0:T(8,128)(2,1)} %bitcast.36, bf16[64,128,768]{2,1,0:T(8,128)(2,1)} %bitcast.37, bf16[64,128,768]{2,1,0:T(8,128)(2,1)} %bitcast.38, ...), custom_call_target="tpu_custom_call" | custom-call | tf_op jit(solution)/shard_map/scores/pallas_call | solution.py:533
  179.9 8.9 %scores.3.mt_ref = f32[40,128,128]{2,1,0:T(8,128)} custom-call(s32[2,40]{1,0:T(2,128)} %pad_add_fusion.index_ref.tmeta.meta, bf16[8,128,768]{2,1,0:T(8,128)(2,1)} %bitcast.48, bf16[64,128,768]{2,1,0:T(8,128)(2,1)} %bitcast.19, bf16[64,128,768]{2,1,0:T(8,128)(2,1)} %bitcast.20, bf16[64,128,768]{2,1,0:T(8,128)(2,1)} %bitcast.21, ...), custom_call_target="tpu_custom_call" | custom-call | tf_op jit(solution)/shard_map/scores/pallas_call | solution.py:533
  188.9 39.9 %fine.1 = (f32[8,128]{1,0:T(8,128)}, f32[8,128]{1,0:T(8,128)}, bf16[32,128,128]{2,1,0:T(8,128)(2,1)}, bf16[40,128,128]{2,1,0:T(8,128)(2,1)}) custom-call(s32[32]{0:T(128)} %get-tuple-element.26.smeta, s32[2,40]{1,0:T(2,128)} %pad_add_fusion.index_ref.tmeta.meta, f32[32,128,128]{2,1,0:T(8,128)} %scores.2.ms_ref, f32[40,128,128]{2,1,0:T(8,128)} %scores.3.mt_ref, ...), custom_call_target="tpu_custom_call" | custom-call | tf_op jit(solution)/shard_map/fine/pallas_call | solution.py:700
  228.8 9.9 %target_mean.1 = bf16[1024,768]{1,0:T(8,128)(2,1)} custom-call(s32[2,40]{1,0:T(2,128)} %pad_add_fusion.index_ref.tmeta.meta, bf16[40,128,128]{2,1,0:T(8,128)(2,1)} %get-tuple-element.17.plan_ref, bf16[64,128,768]{2,1,0:T(8,128)(2,1)} %bitcast.27, bf16[64,128,768]{2,1,0:T(8,128)(2,1)} %bitcast.28, bf16[64,128,768]{2,1,0:T(8,128)(2,1)} %bitcast.29, ...), custom_call_target="tpu_custom_call" | custom-call | tf_op jit(solution)/shard_map/target_mean/pallas_call | solution.py:792
  238.7 0.0 copy-start.4
  238.7 0.0 copy-start.3
  238.7 8.6 %source_mean.1 = bf16[1024,768]{1,0:T(8,128)(2,1)} custom-call(s32[1,32]{1,0:T(1,128)} %fusion.1.index_ref.meta, bf16[32,128,128]{2,1,0:T(8,128)(2,1)} %get-tuple-element.16.plan_ref, bf16[64,128,768]{2,1,0:T(8,128)(2,1)} %bitcast.43, bf16[64,128,768]{2,1,0:T(8,128)(2,1)} %bitcast.44, bf16[64,128,768]{2,1,0:T(8,128)(2,1)} %bitcast.45, ...), custom_call_target="tpu_custom_call" | custom-call | tf_op jit(solution)/shard_map/source_mean/pallas_call | solution.py:745
  247.3 0.0 copy-done.4
  247.3 0.6 copy.29
  247.9 0.0 copy-done.3
  247.9 0.6 copy.30
  (4 shorter events, 0.0 us)
Async XLA Ops:
  0.6 5.1 %copy-start = (bf16[1024,768]{1,0:T(8,128)(2,1)S(1)}, bf16[1024,768]{1,0:T(8,128)(2,1)}, u32[]{:S(2)}) copy-start(bf16[1024,768]{1,0:T(8,128)(2,1)} %y_ref.1) | copy-start | bytes 4718596
  0.6 6.0 %copy-start.2 = (bf16[256,768]{1,0:T(8,128)(2,1)S(1)}, bf16[256,768]{1,0:T(8,128)(2,1)}, u32[]{:S(2)}) copy-start(bf16[256,768]{1,0:T(8,128)(2,1)} %param.12) | copy-start | bytes 1179652
  3.9 4.0 %copy-start.1 = (bf16[1024,192]{0,1:T(8,128)(2,1)S(1)}, bf16[1024,192]{0,1:T(8,128)(2,1)}, u32[]{:S(2)}) copy-start(bf16[1024,192]{0,1:T(8,128)(2,1)} %param.13) | copy-start | bytes 1179652
  238.7 8.6 %copy-start.4 = (f32[8,128]{1,0:T(8,128)S(1)}, f32[8,128]{1,0:T(8,128)}, u32[]{:S(2)}) copy-start(f32[8,128]{1,0:T(8,128)} %get-tuple-element.18) | copy-start | bytes 12292
  238.7 9.2 %copy-start.3 = (f32[8,128]{1,0:T(8,128)S(1)}, f32[8,128]{1,0:T(8,128)}, u32[]{:S(2)}) copy-start(f32[8,128]{1,0:T(8,128)} %get-tuple-element.19) | copy-start | bytes 12292
